TPU v7x, 32 devices: a whole 2x2x4 slice. The times are simulated.
32 devices in a mesh: grp: 16 (over z, y, x), tp: 2 (over core).
Axes of the slice: x: 2, y: 2, z: 4, core: 2. Of those that a mesh axis runs over, the one named last changes fastest.
Arguments:
- qkv: bfloat16 [3, 16384, 1408], P(None, 'grp', 'tp'), as said below
- segments: int32 [16, 1024], P('grp'), may hold values from 0 to 255, as said below
- links: int32 [16], P('grp'), may hold values 0 or 1
- owners: int32 [16, 16, 1], P('grp'), may hold values from 0 to 15; in each aligned block of 16 rows (0 to 15, 16 to 31, ..., all dimensions but the last counted through in order) at most 2 rows name the same one
- merge_weight: bfloat16 [4, 1408, 1408], P(None, 'tp'), may hold values from -0.078125 to 0.078125
- norm_gain: float32 [1408], replicated, may hold values from 0.1 to 1.9
- norm_bias: float32 [1408], replicated, may hold values from -3 to 3
- next_weight: bfloat16 [1408, 4224], P(None, 'tp'), may hold values from -0.15625 to 0.15625
Outputs:
- next_qkv: bfloat16 [16, 512, 4224], P('grp', None, 'tp')
Inputs may be any that keep to these rules, and one draw needn't show every extreme that they name: `qkv`: entries lie within -6 to 6. Within a row ids start at 0 and never fall; the 4 patches of one merged window share an id; a row has three or more segments; its first and its last segment hold at most 256 patches each, and in some row the first, in some row the last, holds exactly 256. `owners`: in each group's 16 blocks no owner appears more than 2 times, and some owner appears exactly 2 times.
All inputs are finite; a program needn't handle non-finite values. No bound on the sum of `links` on one device may be relied on, other than what follows from the above.
Results may differ from a plain program's by a relative error of at most 0.0062.
Values may be sent and summed in bfloat16 or wider, within the bound.
A program may use at most 192 MiB of HBM per device.

v0:
```python
import math

import jax
import jax.numpy as jnp
from jax import lax
from jax.sharding import PartitionSpec as P

DH = 88
WIN = 4
CAP = 2


def shifted(block, axis, distance):
    devices = range(lax.axis_size(axis))
    route = [(i - distance, i) for i in devices if i - distance in devices]
    return lax.ppermute(block, axis, route)


def body(qkv, segments, links, owners, merge_weight, norm_gain, norm_bias, next_weight):
    row_len = qkv.shape[1]
    shard_width = qkv.shape[2]
    head_count = shard_width // DH
    model_width = norm_gain.shape[0]
    score_scale = 1.0 / math.sqrt(DH)
    seg_ids = segments[0]
    in_first = seg_ids == seg_ids[0]
    in_last = seg_ids == seg_ids[row_len - 1]
    linked = links[0] > 0
    sent_rows = row_len // 4
    tail_flag = jnp.logical_and(in_last, linked).astype(jnp.bfloat16)[row_len - sent_rows :]
    front_flag = in_first.astype(jnp.bfloat16)[:sent_rows]
    prev_pairs, prev_flag = shifted((qkv[1:3, row_len - sent_rows :], tail_flag), "grp", 1)
    next_pairs, next_flag = shifted((qkv[1:3, :sent_rows], front_flag), "grp", -1)
    all_keys = jnp.concatenate([prev_pairs[0], qkv[1], next_pairs[0]], axis=0)
    key_total = all_keys.shape[0]
    all_keys = all_keys.reshape(key_total, head_count, DH)
    all_values = jnp.concatenate([prev_pairs[1], qkv[2], next_pairs[1]], axis=0).reshape(
        key_total, head_count, DH
    )
    prev_ok = prev_flag > 0
    next_ok = jnp.logical_and(next_flag > 0, linked)
    query_len = min(512, row_len)
    query_blocks = qkv[0].reshape(row_len // query_len, query_len, head_count, DH)
    seg_blocks = seg_ids.reshape(row_len // query_len, query_len)

    def attend(block_inputs):
        queries, query_seg = block_inputs
        same_seg = query_seg[:, None] == seg_ids[None, :]
        prev_pass = jnp.logical_and((query_seg == seg_ids[0])[:, None], prev_ok[None, :])
        next_pass = jnp.logical_and((query_seg == seg_ids[row_len - 1])[:, None], next_ok[None, :])
        allowed = jnp.concatenate([prev_pass, same_seg, next_pass], axis=1)
        scores = (
            jnp.einsum("qhd,khd->hqk", queries, all_keys, preferred_element_type=jnp.float32)
            * score_scale
        )
        scores = jnp.where(allowed[None], scores, -jnp.inf)
        row_max = jnp.max(scores, axis=2, keepdims=True)
        exp_scores = jnp.exp(scores - row_max)
        weights = (exp_scores / jnp.sum(exp_scores, axis=2, keepdims=True)).astype(jnp.bfloat16)
        attended_block = jnp.einsum(
            "hqk,khd->qhd", weights, all_values, preferred_element_type=jnp.float32
        )
        return attended_block.astype(jnp.bfloat16).reshape(query_len, head_count * DH)

    attended = lax.map(attend, (query_blocks, seg_blocks)).reshape(row_len, shard_width)
    merged_rows = row_len // WIN
    partial_sum = jnp.dot(
        attended.reshape(merged_rows, WIN * shard_width),
        merge_weight.reshape(WIN * shard_width, model_width),
        preferred_element_type=jnp.float32,
    )
    merged = lax.psum(partial_sum, "tp")
    feature_sum = jnp.sum(merged, axis=1, keepdims=True)
    square_sum = jnp.sum(merged * merged, axis=1, keepdims=True)
    feature_mean = feature_sum / model_width
    variance = square_sum / model_width - feature_mean * feature_mean
    normed = ((merged - feature_mean) * lax.rsqrt(variance + 1e-05) * norm_gain + norm_bias).astype(
        jnp.bfloat16
    )
    owner_ids = owners[0, :, 0]
    block_count = owner_ids.shape[0]
    group_count = lax.axis_size("grp")
    block_index = jnp.arange(block_count)
    earlier = block_index[:, None] > block_index[None, :]
    slot_rank = jnp.sum(
        jnp.logical_and(owner_ids[:, None] == owner_ids[None, :], earlier).astype(jnp.int32), axis=1
    )
    target = owner_ids * CAP + slot_rank
    placing = (target[:, None] == jnp.arange(group_count * CAP)[None, :]).astype(jnp.bfloat16)
    block_rows = merged_rows // block_count
    feature_count = normed.shape[1]
    packed = jnp.einsum(
        "bs,bf->sf",
        placing,
        normed.reshape(block_count, block_rows * feature_count),
        preferred_element_type=jnp.float32,
    )
    packed = packed.astype(jnp.bfloat16).reshape(group_count, CAP * block_rows, feature_count)
    projected = jnp.einsum(
        "hom,mr->hor",
        lax.all_to_all(packed, "grp", split_axis=0, concat_axis=0, tiled=True),
        next_weight,
        preferred_element_type=jnp.float32,
    ).astype(jnp.bfloat16)
    return projected.reshape(1, group_count * CAP * block_rows, projected.shape[2])


def solution(mesh):
    placed = (
        P(None, "grp", "tp"),
        P("grp", None),
        P("grp"),
        P("grp", None, None),
        P(None, "tp", None),
        P(),
        P(),
        P(None, "tp"),
    )
    return jax.shard_map(
        body, mesh=mesh, in_specs=placed, out_specs=P("grp", None, "tp"), check_vma=False
    )
```

profile of v0, /device:TPU:0, one launch (start us, length us, event | category | flops | bytes accessed | tf_op | source)
XLA Modules:
  0.0 195.9 jit_solution(11463710172644740484)
XLA Ops:
  6.5 2.5 %fusion.47 = (bf16[2,256,704]{1,2,0:T(8,128)(2,1)}, bf16[2,256,704]{1,2,0:T(8,128)(2,1)}) fusion(bf16[3,1024,704]{1,2,0:T(8,128)(2,1)} %param.10), kind=kLoop, calls=%fused_computation.57 | loop fusion | bytes 2883584 | tf_op jit(solution)/shard_map/slice | solution.py:32
  9.1 5.7 %collective-permute-start.2 = (bf16[2,256,704]{1,2,0:T(8,128)(2,1)}, bf16[2,256,704]{1,2,0:T(8,128)(2,1)}, u32[]{:S(2)}, u32[]{:S(2)}) collective-permute-start(bf16[2,256,704]{1,2,0:T(8,128)(2,1)} %get-tuple-element.109), channel_id=1, source_target_pairs={{0,2},{2,4},{4,6},{6,8},{8,10},{10,12},{12,14},{14,16},{16,18},{18... | collective-permute-start | bytes 2162696 | tf_op jit(solution)/shard_map/ppermute | solution.py:16
  14.8 1.3 collective-permute-start.3
  16.1 0.6 fusion.50
  17.3 1.2 broadcast_compare_fusion.3
  18.5 1.3 collective-permute-start.1
  19.9 5.2 %collective-permute-start = (bf16[256]{0:T(256)(128)(2,1)S(1)}, bf16[256]{0:T(256)(128)(2,1)S(1)}, u32[]{:S(2)}, u32[]{:S(2)}) collective-permute-start(bf16[256]{0:T(256)(128)(2,1)S(1)} %slice_convert_fusion.1), channel_id=1, source_target_pairs={{0,2},{2,4},{4,6},{6,8},{8,10},{10,12},{12,14},{14,16},{16,18},{18... | collective-permute-start | bytes 1544 | tf_op jit(solution)/shard_map/ppermute | solution.py:16
  25.0 4.3 %fusion.46 = (bf16[1,1024,704]{1,2,0:T(8,128)(2,1)}, bf16[1,1024,704]{1,2,0:T(8,128)(2,1)}, bf16[1,1024,704]{1,2,0:T(8,128)(2,1)S(1)}) fusion(bf16[3,1024,704]{1,2,0:T(8,128)(2,1)} %param.10), kind=kLoop, calls=%fused_computation.56 | loop fusion | bytes 8650752 | tf_op jit(solution)/shard_map/slice | solution.py:37
  29.3 1.1 reshape_squeeze.7
  30.4 1.3 copy.13
  31.7 0.5 broadcast.73
  32.3 0.8 reduce.3
  33.1 13.9 %collective-permute-done.1 = bf16[256]{0:T(256)(128)(2,1)S(1)} collective-permute-done((bf16[256]{0:T(256)(128)(2,1)S(1)}, bf16[256]{0:T(256)(128)(2,1)S(1)}, u32[]{:S(2)}, u32[]{:S(2)}) %collective-permute-start.1) | collective-permute-done | bytes 544 | tf_op jit(solution)/shard_map/ppermute | solution.py:16
  47.1 1.1 fusion.48
  48.2 1.1 fusion.49
  49.4 2.3 %pad_maximum_fusion = (bf16[1536,8,88]{0,2,1:T(8,128)(2,1)}, bf16[1536,8,88]{0,2,1:T(8,128)(2,1)}) fusion(bf16[256,8,88]{0,2,1:T(8,128)(2,1)S(1)} %bitcast.78, bf16[1024,8,88]{0,2,1:T(8,128)(2,1)S(1)} %bitcast.73, bf16[256,8,88]{0,2,1:T(8,128)(2,1)S(1)} %bitcast.76, bf16[256,8,88]{0,2,1:T(8,128)(2,1)S(1)} %bitcast.77, bf16[1024,8,88]{0,2,1:T(8,128)(2,1)S(1)} %bitcast.72, ...), kind=kLoop, calls=%fused_computation.35 | loop fusion | flops 12976128 | bytes 8650752 | tf_op jit(solution)/shard_map/concatenate | solution.py:34
  51.7 51.4 %while.10 = (s32[]{:T(128)}, bf16[2,512,704]{1,2,0:T(8,128)(2,1)}, s32[2,512]{1,0:T(2,128)S(1)}, s32[1024]{0:T(1024)S(1)}, pred[256]{0:T(512)(128)(4,1)S(1)}, /*...) while((s32[]{:T(128)}, bf16[2,512,704]{1,2,0:T(8,128)(2,1)}, ...), condition=%wide.region_4.5_spmd, body=%wide.region_1.0_spmd.sunk | while | flops 3381239808 | bytes 34258656 | solution.py:65
  51.7 0.6 fusion.72
  52.3 1.3 broadcast_compare_fusion.7
  53.6 0.2 broadcast_and_fusion.3
  53.8 0.4 broadcast_compare_fusion.8
  54.2 0.1 pad_add_fusion.2
  54.3 9.2 %fusion.73 = f32[8,512]{1,0:T(8,128)S(1)} fusion(pred[512,1536]{1,0:T(8,128)(4,1)S(1)} %pad_add_fusion.2, bf16[1536,8,88]{0,2,1:T(8,128)(2,1)S(1)} %copy-done.3, bf16[2,512,8,88]{1,3,2,0:T(8,128)(2,1)} %get-tuple-element.225, s32[]{:T(128)} %get-tuple-element.207), kind=kOutput, calls=%fused_computation.55.clone.1 | convolution fusion | flops 1132463616 | bytes 3686912 | tf_op jit(solution)/shard_map/while/body/eval_jaxpr/sub | solution.py:58
  63.5 12.7 %fusion.74 = bf16[8,512,88]{1,2,0:T(8,128)(2,1)S(1)} fusion(bf16[1536,8,88]{0,2,1:T(8,128)(2,1)} %get-tuple-element.227, f32[8,512]{1,0:T(8,128)S(1)} %fusion.73, pred[512,1536]{1,0:T(8,128)(4,1)S(1)} %pad_add_fusion.2, bf16[1536,8,88]{0,2,1:T(8,128)(2,1)} %get-tuple-element.226, bf16[2,512,8,88]{1,3,2,0:T(8,128)(2,1)} %get-tuple-element.225, ...), kind=kOutput, calls=%fused_computation.10.clone.1 | convolution fusion | flops 2246415872 | bytes 6570496 | tf_op jit(solution)/shard_map/while/body/eval_jaxpr/hqk,khd->qhd/dot_general | solution.py:60
  76.2 0.1 bitcast_dynamic-update-slice_fusion.2
  76.3 1.1 copy-done.5
  77.4 0.6 fusion.72
  78.0 1.3 broadcast_compare_fusion.7
  79.3 0.2 broadcast_and_fusion.3
  79.5 0.4 broadcast_compare_fusion.8
  79.8 0.1 pad_add_fusion.2
  79.9 9.2 %fusion.73 = f32[8,512]{1,0:T(8,128)S(1)} fusion(pred[512,1536]{1,0:T(8,128)(4,1)S(1)} %pad_add_fusion.2, bf16[1536,8,88]{0,2,1:T(8,128)(2,1)S(1)} %copy-done.3, bf16[2,512,8,88]{1,3,2,0:T(8,128)(2,1)} %get-tuple-element.225, s32[]{:T(128)} %get-tuple-element.207), kind=kOutput, calls=%fused_computation.55.clone.1 | convolution fusion | flops 1132463616 | bytes 3686912 | tf_op jit(solution)/shard_map/while/body/eval_jaxpr/sub | solution.py:58
  89.2 12.7 %fusion.74 = bf16[8,512,88]{1,2,0:T(8,128)(2,1)S(1)} fusion(bf16[1536,8,88]{0,2,1:T(8,128)(2,1)} %get-tuple-element.227, f32[8,512]{1,0:T(8,128)S(1)} %fusion.73, pred[512,1536]{1,0:T(8,128)(4,1)S(1)} %pad_add_fusion.2, bf16[1536,8,88]{0,2,1:T(8,128)(2,1)} %get-tuple-element.226, bf16[2,512,8,88]{1,3,2,0:T(8,128)(2,1)} %get-tuple-element.225, ...), kind=kOutput, calls=%fused_computation.10.clone.1 | convolution fusion | flops 2246415872 | bytes 6570496 | tf_op jit(solution)/shard_map/while/body/eval_jaxpr/hqk,khd->qhd/dot_general | solution.py:60
  101.9 0.1 bitcast_dynamic-update-slice_fusion.2
  101.9 1.1 copy-done.5
  103.1 1.7 copy.14
  104.7 1.7 reshape_reshape.3
  106.4 6.8 %fusion.51 = f32[256,1408]{1,0:T(8,128)} fusion(bf16[256,2816]{1,0:T(8,128)(2,1)S(1)} %reshape_reshape.3, bf16[2816,1408]{1,0:T(8,128)(2,1)} %bitcast.86), kind=kOutput, calls=%fused_computation.61 | convolution fusion | flops 2030043136 | bytes 10813440 | tf_op jit(solution)/shard_map/dot_general | solution.py:67
  113.2 0.2 convert_reduce_fusion
  113.4 20.5 %all-reduce.2.cloned.1.call-done = f32[256,1408]{1,0:T(8,128)} async-done(((f32[256,1408]{1,0:T(8,128)}), f32[256,1408]{1,0:T(8,128)}) %all-reduce.2.cloned.1.call-update) | async-done | bytes 1441808 | tf_op jit(solution)/shard_map/psum | solution.py:72
  133.9 1.7 fusion.41
  135.7 0.3 add_convert_fusion
  136.0 0.3 reshape.82
  136.4 0.6 convolution_convert_fusion
  137.0 0.7 reshape.83
  137.7 42.1 %all_to_all.5 = bf16[16,32,1408]{2,1,0:T(8,128)(2,1)S(1)} all-to-all(bf16[16,32,1408]{2,1,0:T(8,128)(2,1)S(1)} %reshape.83), channel_id=1, replica_groups=mesh['grp'=16,'tp'=2] {'grp'}, dimensions={0} | all-to-all | bytes 2883584 | tf_op jit(solution)/shard_map/all_to_all | solution.py:101
  179.8 6.8 %fusion.36 = bf16[16,32,2112]{2,1,0:T(8,128)(2,1)S(1)} fusion(bf16[16,32,1408]{2,1,0:T(8,128)(2,1)S(1)} %all_to_all.5, bf16[1408,2112]{0,1:T(8,128)(2,1)} %param.17), kind=kOutput, calls=%fused_computation.34 | convolution fusion | flops 3046146048 | bytes 9551872 | tf_op jit(solution)/shard_map/hom,mr->hor/dot_general | solution.py:99
  186.6 2.4 %copy.15 = bf16[1,512,2112]{1,2,0:T(8,128)(2,1)} copy(bf16[1,512,2112]{2,1,0:T(8,128)(2,1)S(1)} %bitcast.74) | data formatting | bytes 4325376 | tf_op jit(solution)/shard_map/reshape | solution.py:105
  (39 shorter events, 0.2 us)
Async XLA Ops:
  6.5 9.6 %copy-start.6 = (s32[1,1024]{1,0:T(1,128)S(1)}, s32[1,1024]{1,0:T(1,128)}, u32[]{:S(2)}) copy-start(s32[1,1024]{1,0:T(1,128)} %param.11) | copy-start | bytes 12292
  6.5 127.4 %all-reduce.2.cloned.1.call-start = ((), (), s32[]{:S(2)}) async-start(), calls=%async_computation.1 | async-start | bytes 2883584 | tf_op jit(solution)/shard_map/psum | solution.py:72
  9.1 38.0 %collective-permute-start.2 = (bf16[2,256,704]{1,2,0:T(8,128)(2,1)}, bf16[2,256,704]{1,2,0:T(8,128)(2,1)}, u32[]{:S(2)}, u32[]{:S(2)}) collective-permute-start(bf16[2,256,704]{1,2,0:T(8,128)(2,1)} %get-tuple-element.109), channel_id=1, source_target_pairs={{0,2},{2,4},{4,6},{6,8},{8,10},{10,12},{12,14},{14,16},{16,18},{18... | collective-permute-start | bytes 2162696 | tf_op jit(solution)/shard_map/ppermute | solution.py:16
  14.8 33.4 %collective-permute-start.3 = (bf16[2,256,704]{1,2,0:T(8,128)(2,1)}, bf16[2,256,704]{1,2,0:T(8,128)(2,1)}, u32[]{:S(2)}, u32[]{:S(2)}) collective-permute-start(bf16[2,256,704]{1,2,0:T(8,128)(2,1)} %get-tuple-element.110), channel_id=1, source_target_pairs={{2,0},{4,2},{6,4},{8,6},{10,8},{12,10},{14,12},{16,14},{18,16},{20... | collective-permute-start | bytes 2162696 | tf_op jit(solution)/shard_map/ppermute | solution.py:16
  18.5 28.5 %collective-permute-start.1 = (bf16[256]{0:T(256)(128)(2,1)S(1)}, bf16[256]{0:T(256)(128)(2,1)S(1)}, u32[]{:S(2)}, u32[]{:S(2)}) collective-permute-start(bf16[256]{0:T(256)(128)(2,1)S(1)} %slice_convert_fusion), channel_id=1, source_target_pairs={{2,0},{4,2},{6,4},{8,6},{10,8},{12,10},{14,12},{16,14},{18,16},{20... | collective-permute-start | bytes 1544 | tf_op jit(solution)/shard_map/ppermute | solution.py:16
  19.9 27.2 %collective-permute-start = (bf16[256]{0:T(256)(128)(2,1)S(1)}, bf16[256]{0:T(256)(128)(2,1)S(1)}, u32[]{:S(2)}, u32[]{:S(2)}) collective-permute-start(bf16[256]{0:T(256)(128)(2,1)S(1)} %slice_convert_fusion.1), channel_id=1, source_target_pairs={{0,2},{2,4},{4,6},{6,8},{8,10},{10,12},{12,14},{14,16},{16,18},{18... | collective-permute-start | bytes 1544 | tf_op jit(solution)/shard_map/ppermute | solution.py:16
  31.7 17.6 %copy-start.1 = (bf16[1,1024,704]{1,2,0:T(8,128)(2,1)S(1)}, bf16[1,1024,704]{1,2,0:T(8,128)(2,1)}, u32[]{:S(2)}) copy-start(bf16[1,1024,704]{1,2,0:T(8,128)(2,1)} %get-tuple-element.106) | copy-start | bytes 4325380
  31.7 17.6 %copy-start.2 = (bf16[1,1024,704]{1,2,0:T(8,128)(2,1)S(1)}, bf16[1,1024,704]{1,2,0:T(8,128)(2,1)}, u32[]{:S(2)}) copy-start(bf16[1,1024,704]{1,2,0:T(8,128)(2,1)} %get-tuple-element.107) | copy-start | bytes 4325380
  51.7 2.6 %copy-start.3 = (bf16[1536,8,88]{0,2,1:T(8,128)(2,1)S(1)}, bf16[1536,8,88]{0,2,1:T(8,128)(2,1)}, u32[]{:S(2)}) copy-start(bf16[1536,8,88]{0,2,1:T(8,128)(2,1)} %get-tuple-element.226) | copy-start | bytes 6488068 | tf_op jit(solution)/shard_map/while
  63.5 12.7 %copy-start.4 = (bf16[2,512,704]{1,2,0:T(8,128)(2,1)S(1)}, bf16[2,512,704]{1,2,0:T(8,128)(2,1)}, u32[]{:S(2)}) copy-start(bf16[2,512,704]{1,2,0:T(8,128)(2,1)} %get-tuple-element.208) | copy-start | bytes 4325380 | tf_op jit(solution)/shard_map/while
  76.2 1.1 copy-start.5
  77.4 2.6 %copy-start.3 = (bf16[1536,8,88]{0,2,1:T(8,128)(2,1)S(1)}, bf16[1536,8,88]{0,2,1:T(8,128)(2,1)}, u32[]{:S(2)}) copy-start(bf16[1536,8,88]{0,2,1:T(8,128)(2,1)} %get-tuple-element.226) | copy-start | bytes 6488068 | tf_op jit(solution)/shard_map/while
  89.2 12.7 %copy-start.4 = (bf16[2,512,704]{1,2,0:T(8,128)(2,1)S(1)}, bf16[2,512,704]{1,2,0:T(8,128)(2,1)}, u32[]{:S(2)}) copy-start(bf16[2,512,704]{1,2,0:T(8,128)(2,1)} %get-tuple-element.208) | copy-start | bytes 4325380 | tf_op jit(solution)/shard_map/while
  101.9 1.1 copy-start.5
  106.4 6.8 %copy-start.9 = (s32[1,16,1]{1,2,0:T(1,128)S(1)}, s32[1,16,1]{1,2,0:T(1,128)}, u32[]{:S(2)}) copy-start(s32[1,16,1]{1,2,0:T(1,128)} %param.13) | copy-start | bytes 196
  113.2 22.5 %copy-start.7 = (f32[1408]{0:T(1024)S(1)}, f32[1408]{0:T(1024)}, u32[]{:S(2)}) copy-start(f32[1408]{0:T(1024)} %param.16) | copy-start | bytes 16900
  113.2 22.5 %copy-start.8 = (f32[1408]{0:T(1024)S(1)}, f32[1408]{0:T(1024)}, u32[]{:S(2)}) copy-start(f32[1408]{0:T(1024)} %param.15) | copy-start | bytes 16900
  133.9 1.8 copy-start
Sparse Core Ops, SparseCore 0:
  113.4 20.5 all-reduce.1
where the time goes:
time: 196 us
  matrix products  58 us (30%)
  blocking collectives  42.1 us (21%)
  waiting for transfers between devices  34.4 us (18%)
  local copies, waits for them, and re-layouts  23 us (12%)
  between operations  14.3 us (7%)
  starting transfers between devices  13.5 us (7%)
  other arithmetic  10.5 us (5%)
    all_to_all x1, blocking collectives, body(): lax.all_to_all(packed, 'grp', split_axis=0, concat_axis=0, tiled=True)  42.1 us
    dot_general x2, matrix products, attend(): jnp.einsum('hqk,khd->qhd', weights, all_values, preferred_element_type=jn...  25.3 us
    psum x1, waiting for transfers between devices, body(): merged = lax.psum(partial_sum, 'tp')  20.5 us
    sub x2, matrix products, attend(): exp_scores = jnp.exp(scores - row_max)  18.5 us
    ppermute x4, waiting for transfers between devices, shifted(): return lax.ppermute(block, axis, route)  13.9 us
    ppermute x4, starting transfers between devices, shifted(): return lax.ppermute(block, axis, route)  13.5 us
    dot_general x1, matrix products, body(): jnp.einsum('hom,mr->hor', lax.all_to_all(packed, 'grp', split_axis=0, con...  6.78 us
    dot_general x1, matrix products, body(): jnp.dot(attended.reshape(merged_rows, WIN * shard_width), merge_weight.re...  6.76 us
  transfers between devices with their start and end apart: 5, of which 2 were waited for; matrix products, arithmetic and copies ran while one was open for 6% of the time, Pallas kernels for 0%

commit v1 on v0

v1 whole, which is shorter than its diff:
```python
import functools
import math

import jax
import jax.numpy as jnp
from jax import lax
from jax.experimental import pallas as pl
from jax.experimental.pallas import tpu as pltpu
from jax.sharding import PartitionSpec as P

DH = 88
WIN = 4
CAP = 2
TILE = 128
EPS = 1e-05
NEG = -1e30
SCALE2 = math.log2(math.e) / math.sqrt(DH)


def shifted(block, axis, distance):
    devices = range(lax.axis_size(axis))
    route = [(i - distance, i) for i in devices if i - distance in devices]
    return lax.ppermute(block, axis, route)


def swapped(block, axis):
    return lax.ppermute(block, axis, [(0, 1), (1, 0)])


def windows(width):
    spans = []
    for head in range(width // DH):
        low, high = head * DH, head * DH + DH
        spans.append((low, high, low // TILE * TILE, min(width, -(-high // TILE) * TILE)))
    return spans


def head_mask(low, high, start, stop):
    column = start + lax.broadcasted_iota(jnp.int32, (1, stop - start), 1)
    return jnp.logical_and(column >= low, column < high)


def attend_heads(width, read_query, key_parts, bias_parts, value_parts, write):
    pieces = {}
    for low, high, start, stop in windows(width):
        mask = head_mask(low, high, start, stop)
        query = read_query(start, stop) * mask.astype(jnp.float32).astype(jnp.bfloat16)
        scores = [
            lax.dot_general(
                query, keys(start, stop), (((1,), (1,)), ((), ())), preferred_element_type=jnp.float32
            )
            * SCALE2
            + bias
            for keys, bias in zip(key_parts, bias_parts)
        ]
        top = jnp.max(scores[0], axis=1, keepdims=True)
        for part in scores[1:]:
            top = jnp.maximum(top, jnp.max(part, axis=1, keepdims=True))
        weights = [jnp.exp2(part - top) for part in scores]
        total = jnp.sum(weights[0], axis=1, keepdims=True)
        for part in weights[1:]:
            total = total + jnp.sum(part, axis=1, keepdims=True)
        mixed = None
        for part, values in zip(weights, value_parts):
            term = jnp.dot(
                part.astype(jnp.bfloat16), values(start, stop), preferred_element_type=jnp.float32
            )
            mixed = term if mixed is None else mixed + term
        mixed = mixed * (1.0 / total)
        for at in range(start, stop, TILE):
            end = min(at + TILE, stop)
            piece = mixed[:, at - start : end - start]
            if at in pieces:
                piece = jnp.where(head_mask(low, high, at, end), piece, pieces[at])
            pieces[at] = piece
            if high >= end:
                write(at, end, pieces[at].astype(jnp.bfloat16))


def attention_kernel(edge, row_len, width, sent, *refs):
    if edge:
        seg_smem, counts, qkv, seg_row, seg_col, prev, following, out = refs
    else:
        seg_smem, qkv, seg_row, seg_col, out = refs
    tiles = row_len // TILE
    edge_tiles = sent // TILE

    def one(tile, out_row, neighbour):
        first = seg_smem[0, tile * TILE]
        last = seg_smem[0, tile * TILE + TILE - 1]
        begin, stop = jnp.int32(0), jnp.int32(0)
        for other in range(tiles):
            begin += (seg_smem[0, other * TILE + TILE - 1] < first).astype(jnp.int32)
            stop += (seg_smem[0, other * TILE] <= last).astype(jnp.int32)
        needed = stop - begin
        query_at = pl.multiple_of(tile * TILE, TILE)
        query_ids = seg_col[pl.ds(query_at, TILE), :]

        def run(count):
            key_tile = jnp.minimum(begin, tiles - count)
            key_at = pl.multiple_of(key_tile * TILE, TILE)
            ids = jnp.concatenate([seg_row[pl.ds(key_tile + i, 1), :] for i in range(count)], axis=1)
            bias_parts = [jnp.where(query_ids == ids, 0.0, NEG)]
            key_parts = [lambda a, b: qkv[1, pl.ds(key_at, count * TILE), a:b]]
            value_parts = [lambda a, b: qkv[2, pl.ds(key_at, count * TILE), a:b]]
            if neighbour is not None:
                source, allowed = neighbour
                bias_parts.append(jnp.where(allowed, 0.0, NEG))
                key_parts.append(lambda a, b: source[0, :sent, a:b])
                value_parts.append(lambda a, b: source[1, :sent, a:b])

            def write(a, b, value):
                out[pl.ds(out_row, TILE), a:b] = value

            attend_heads(
                width,
                lambda a, b: qkv[0, pl.ds(query_at, TILE), a:b],
                key_parts,
                bias_parts,
                value_parts,
                write,
            )

        sizes = [size for size in (2, 3, 4) if size < tiles] + [tiles]
        floor = 0
        for size in sizes:
            pl.when(jnp.logical_and(needed > floor, needed <= size))(functools.partial(run, size))
            floor = size

    if not edge:
        @pl.loop(edge_tiles, tiles - edge_tiles)
        def _(tile):
            one(tile, pl.multiple_of((tile - edge_tiles) * TILE, TILE), None)
        return

    slot = lax.broadcasted_iota(jnp.int32, (1, sent), 1)

    @pl.loop(0, edge_tiles)
    def _(tile):
        at = pl.multiple_of(tile * TILE, TILE)
        rows = seg_col[pl.ds(at, TILE), :]
        ok = jnp.logical_and(rows == seg_smem[0, 0], slot >= sent - counts[0])
        one(tile, at, (prev, ok))

    @pl.loop(0, edge_tiles)
    def _(step):
        tile = tiles - edge_tiles + step
        rows = seg_col[pl.ds(pl.multiple_of(tile * TILE, TILE), TILE), :]
        ok = jnp.logical_and(rows == seg_smem[0, row_len - 1], slot < counts[1])
        one(tile, pl.multiple_of((edge_tiles + step) * TILE, TILE), (following, ok))


def run_attention(edge, qkv, segments, sent, extra):
    row_len, width = qkv.shape[1:]
    rows = 2 * sent if edge else row_len - 2 * sent
    smem = pl.BlockSpec(memory_space=pltpu.SMEM)
    vmem = pl.BlockSpec(memory_space=pltpu.VMEM)
    operands = [segments]
    specs = [smem]
    if edge:
        operands.append(extra[0])
        specs.append(smem)
    operands += [qkv, segments.reshape(row_len // TILE, TILE), segments.reshape(row_len, 1)]
    specs += [vmem] * 3
    if edge:
        operands += [extra[1], extra[2]]
        specs += [vmem] * 2
    return pl.pallas_call(
        functools.partial(attention_kernel, edge, row_len, width, sent),
        out_shape=jax.ShapeDtypeStruct((rows, width), jnp.bfloat16),
        in_specs=specs,
        out_specs=vmem,
        compiler_params=pltpu.CompilerParams(vmem_limit_bytes=40 << 20),
        cost_estimate=pl.CostEstimate(
            flops=rows * 512 * width * 6, bytes_accessed=qkv.size * 2, transcendentals=rows * 512 * 8
        ),
        name="edge_attention" if edge else "middle_attention",
    )(*operands)


def norm_pack_kernel(width, mine_ref, other_ref, gain_ref, bias_ref, target_ref, half_ref, out_ref):
    merged = mine_ref[...] + other_ref[...]
    model_width = merged.shape[1]
    mean = jnp.sum(merged, axis=1, keepdims=True) / model_width
    variance = jnp.sum(merged * merged, axis=1, keepdims=True) / model_width - mean * mean
    normed = (merged - mean) * lax.rsqrt(variance + EPS) * gain_ref[...] + bias_ref[...]
    normed = normed.astype(jnp.bfloat16)
    left, right = normed[:, :width], normed[:, width:]
    place = lax.broadcasted_iota(jnp.int32, (out_ref.shape[0], merged.shape[0]), 0)
    place = jnp.where(place == target_ref[...], 1.0, 0.0).astype(jnp.bfloat16)
    half = half_ref[0]

    @pl.when(half == 0)
    def _():
        out_ref[...] = jnp.dot(place, left, preferred_element_type=jnp.float32).astype(jnp.bfloat16)

    @pl.when(half != 0)
    def _():
        out_ref[...] = jnp.dot(place, right, preferred_element_type=jnp.float32).astype(jnp.bfloat16)


def norm_pack(mine, other, gain, bias, target, half, slots):
    width = mine.shape[1] // 2
    vmem = pl.BlockSpec(memory_space=pltpu.VMEM)
    return pl.pallas_call(
        functools.partial(norm_pack_kernel, width),
        out_shape=jax.ShapeDtypeStruct((slots, width), jnp.bfloat16),
        in_specs=[vmem] * 5 + [pl.BlockSpec(memory_space=pltpu.SMEM)],
        out_specs=vmem,
        compiler_params=pltpu.CompilerParams(vmem_limit_bytes=32 << 20),
        name="norm_pack",
    )(mine, other, gain[None], bias[None], target[None], half)


def body(qkv, segments, links, owners, merge_weight, norm_gain, norm_bias, next_weight):
    row_len = qkv.shape[1]
    shard_width = qkv.shape[2]
    model_width = norm_gain.shape[0]
    tp_size = lax.axis_size("tp")
    seg_ids = segments[0]
    linked = links[0] > 0
    sent = row_len // 4
    last_count = jnp.sum((seg_ids == seg_ids[row_len - 1]).astype(jnp.int32))
    first_count = jnp.sum((seg_ids == seg_ids[0]).astype(jnp.int32))
    last_count = jnp.where(linked, last_count, 0)

    def payload(pairs, count):
        mark = jnp.broadcast_to(count.astype(jnp.bfloat16), (2, 16, shard_width))
        return jnp.concatenate([pairs, mark], axis=1)

    prev = shifted(payload(qkv[1:3, row_len - sent :], last_count), "grp", 1)
    following = shifted(payload(qkv[1:3, :sent], first_count), "grp", -1)
    prev_count = prev[0, sent, 0].astype(jnp.int32)
    next_count = jnp.where(linked, following[0, sent, 0].astype(jnp.int32), 0)
    merge_flat = merge_weight.reshape(WIN * shard_width, model_width)

    def merge(attended):
        return jnp.dot(
            attended.reshape(-1, WIN * shard_width), merge_flat, preferred_element_type=jnp.float32
        )

    middle = merge(run_attention(False, qkv, segments, sent, None))
    edges = merge(
        run_attention(True, qkv, segments, sent, (jnp.stack([prev_count, next_count]), prev, following))
    )
    cut = sent // WIN
    partial_sum = jnp.concatenate([edges[:cut], middle, edges[cut:]], axis=0)
    merged_rows = row_len // WIN

    owner_ids = owners[0, :, 0]
    block_count = owner_ids.shape[0]
    group_count = lax.axis_size("grp")
    block_rows = merged_rows // block_count
    block_index = jnp.arange(block_count)
    earlier = block_index[:, None] > block_index[None, :]
    slot_rank = jnp.sum(
        jnp.logical_and(owner_ids[:, None] == owner_ids[None, :], earlier).astype(jnp.int32), axis=1
    )
    target = (owner_ids * CAP + slot_rank)[:, None] * block_rows + jnp.arange(block_rows)[None, :]
    target = target.reshape(merged_rows)
    slots = group_count * CAP * block_rows

    if tp_size == 2:
        half_index = lax.axis_index("tp")
        other = swapped(partial_sum, "tp")
        packed = norm_pack(
            partial_sum, other, norm_gain, norm_bias, target, half_index[None].astype(jnp.int32), slots
        )
        half_width = model_width // 2
        packed = packed.reshape(group_count, CAP * block_rows, half_width)
        arrived = lax.all_to_all(packed, "grp", split_axis=0, concat_axis=0, tiled=True)
        arrived = arrived.reshape(slots, half_width)
        beside = swapped(arrived, "tp")
        left = jnp.where(half_index == 0, arrived, beside)
        right = jnp.where(half_index == 0, beside, arrived)
        routed = jnp.concatenate([left, right], axis=1)
    else:
        merged = lax.psum(partial_sum, "tp")
        mean = jnp.mean(merged, axis=1, keepdims=True)
        variance = jnp.mean(merged * merged, axis=1, keepdims=True) - mean * mean
        normed = (merged - mean) * lax.rsqrt(variance + EPS) * norm_gain + norm_bias
        normed = normed.astype(jnp.bfloat16)
        placing = (jnp.arange(slots)[:, None] == target[None, :]).astype(jnp.bfloat16)
        packed = jnp.dot(placing, normed, preferred_element_type=jnp.float32).astype(jnp.bfloat16)
        packed = packed.reshape(group_count, CAP * block_rows, model_width)
        routed = lax.all_to_all(packed, "grp", split_axis=0, concat_axis=0, tiled=True)
        routed = routed.reshape(slots, model_width)
    projected = jnp.dot(routed, next_weight, preferred_element_type=jnp.float32)
    return projected.astype(jnp.bfloat16)[None]


def solution(mesh):
    placed = (
        P(None, "grp", "tp"),
        P("grp", None),
        P("grp"),
        P("grp", None, None),
        P(None, "tp", None),
        P(),
        P(),
        P(None, "tp"),
    )
    return jax.shard_map(
        body, mesh=mesh, in_specs=placed, out_specs=P("grp", None, "tp"), check_vma=False
    )
```

time: 196 us -> 123 us (0.63)
  matrix products: 58 us -> 17.9 us
  Pallas kernels: 0 us -> 21.3 us
  waiting for transfers between devices: 34.4 us -> 20.3 us
  blocking collectives: 42.1 us -> 30.6 us
  between operations: 14.3 us -> 3.38 us
  other arithmetic: 10.5 us -> 3.15 us
  starting transfers between devices: 13.5 us -> 6.3 us
  local copies, waits for them, and re-layouts: 23 us -> 20.7 us
    dot_general x5 -> x3, matrix products: 39.5 us -> 17.9 us  [the longest x2 10.3 us: merge(): jnp.dot(attended.reshape(-1, WIN * shard_width), merge_flat, preferred_el...]
    pallas_call x0 -> x3, Pallas kernels: none -> 21.3 us  [the longest x2 20 us: run_attention(): pl.pallas_call(functools.partial(attention_kernel, edge, row_len, width,...]
    psum x1 -> x0, waiting for transfers between devices: 20.5 us -> none  [body(): merged = lax.psum(partial_sum, 'tp')]
    sub x2 -> x0, matrix products: 18.5 us -> none  [attend(): exp_scores = jnp.exp(scores - row_max)]
    all_to_all x1, blocking collectives: 42.1 us -> 30.6 us  [body(): lax.all_to_all(packed, 'grp', split_axis=0, concat_axis=0, tiled=True)]
    unnamed x15, local copies, waits for them, and re-layouts: 0.56 us -> 11.6 us
    ppermute x4 -> x2, starting transfers between devices: 13.5 us -> 6.16 us  [shifted(): return lax.ppermute(block, axis, route)]
    slice x7 -> x5, local copies, waits for them, and re-layouts: 10.9 us -> 3.83 us  [the longest x1 1.49 us: body(): prev = shifted(payload(qkv[1:3, row_len - sent:], last_count), 'grp', 1)]
  transfers between devices with their start and end apart: 5 -> 4, of which waited for: 2 -> 4; matrix products, arithmetic and copies ran while one was open for 6% -> 8% of each run, Pallas kernels for 0% -> 7%
where the time goes in v1:
time: 123 us; the launch traced here: 124 us
  blocking collectives  30.6 us (25%)
  Pallas kernels  21.3 us (17%)
  local copies, waits for them, and re-layouts  20.7 us (17%)
  waiting for transfers between devices  20.3 us (17%)
  matrix products  17.9 us (15%)
  starting transfers between devices  6.3 us (5%)
  between operations  3.38 us (3%)
  other arithmetic  3.15 us (3%)
    all_to_all x1, blocking collectives, body(): lax.all_to_all(packed, 'grp', split_axis=0, concat_axis=0, tiled=True)  30.6 us
    pallas_call x2, Pallas kernels, run_attention(): pl.pallas_call(functools.partial(attention_kernel, edge, row_len, width,...  20 us
    ppermute x2, waiting for transfers between devices, shifted(): return lax.ppermute(block, axis, route)  15.7 us
    unnamed x15, local copies, waits for them, and re-layouts  11.6 us
    dot_general x2, matrix products, merge(): jnp.dot(attended.reshape(-1, WIN * shard_width), merge_flat, preferred_el...  10.3 us
    dot_general x1, matrix products, body(): projected = jnp.dot(routed, next_weight, preferred_element_type=jnp.float32)  7.63 us
    ppermute x2, starting transfers between devices, shifted(): return lax.ppermute(block, axis, route)  6.16 us
    ppermute x2, waiting for transfers between devices, swapped(): return lax.ppermute(block, axis, [(0, 1), (1, 0)])  4.63 us
  transfers between devices with their start and end apart: 4, of which 4 were waited for; matrix products, arithmetic and copies ran while one was open for 8% of the time, Pallas kernels for 7%

profile of v1, /device:TPU:0, one launch (start us, length us, event | category | flops | bytes accessed | tf_op | source)
XLA Modules:
  0.0 123.6 jit_solution(7295188729094730122)
XLA Ops:
  0.0 1.2 %fusion.10 = (s32[1,1]{1,0:T(1,128)}, s32[1,1]{1,0:T(1,128)}) fusion(s32[1,1024]{1,0:T(1,128)} %refs_0_.3), kind=kLoop, calls=%fused_computation.21 | loop fusion | bytes 16 | tf_op jit(solution)/shard_map/slice | solution.py:224
  1.9 2.5 %fusion.5 = (s32[]{:T(128)}, s32[]{:T(128)}) fusion(s32[1,1024]{1,0:T(1,128)} %refs_0_.3, s32[]{:T(128)} %bitcast.1, s32[]{:T(128)} %bitcast.3), kind=kLoop, calls=%fused_computation.14 | loop fusion | flops 6142 | bytes 4112 | tf_op jit(solution)/shard_map/reduce_sum | solution.py:223
  5.1 6.5 %copy.35.refs_2_.refs_1_ = bf16[3,1024,704]{2,1,0:T(8,128)(2,1)} copy(bf16[3,1024,704]{1,2,0:T(8,128)(2,1)} %param.8) | data formatting | bytes 8650752 | tf_op args[0]
  11.6 0.0 copy-start.2
  11.6 1.5 %fusion.8 = (bf16[2,256,704]{2,1,0:T(8,128)(2,1)S(1)}, bf16[2,256,704]{2,1,0:T(8,128)(2,1)S(1)}) fusion(bf16[3,1024,704]{2,1,0:T(8,128)(2,1)} %copy.35.refs_2_.refs_1_), kind=kLoop, calls=%fused_computation.19 | loop fusion | bytes 2883584 | tf_op jit(solution)/shard_map/slice | solution.py:231
  13.1 1.0 concatenate.12
  14.1 4.9 %collective-permute-start = (bf16[2,272,704]{2,1,0:T(8,128)(2,1)}, bf16[2,272,704]{2,1,0:T(8,128)(2,1)S(1)}, u32[]{:S(2)}, u32[]{:S(2)}) collective-permute-start(bf16[2,272,704]{2,1,0:T(8,128)(2,1)} %concatenate.12), channel_id=1, source_target_pairs={{0,2},{2,4},{4,6},{6,8},{8,10},{10,12},{12,14},{14,16},{16,18},{18... | collective-permute-start | bytes 2297864 | tf_op jit(solution)/shard_map/ppermute | solution.py:23
  19.6 1.0 concatenate.13
  20.5 1.3 %collective-permute-start.1 = (bf16[2,272,704]{2,1,0:T(8,128)(2,1)}, bf16[2,272,704]{2,1,0:T(8,128)(2,1)S(1)}, u32[]{:S(2)}, u32[]{:S(2)}) collective-permute-start(bf16[2,272,704]{2,1,0:T(8,128)(2,1)} %concatenate.13), channel_id=1, source_target_pairs={{2,0},{4,2},{6,4},{8,6},{10,8},{12,10},{14,12},{16,14},{18,16},{20... | collective-permute-start | bytes 2297864 | tf_op jit(solution)/shard_map/ppermute | solution.py:23
  21.8 0.0 copy-done.2
  21.8 0.2 copy.38.refs_4_.refs_3_
  22.1 0.0 copy-start
  22.1 2.3 %copy-done = bf16[3,1024,704]{2,1,0:T(8,128)(2,1)S(1)} copy-done((bf16[3,1024,704]{2,1,0:T(8,128)(2,1)S(1)}, bf16[3,1024,704]{2,1,0:T(8,128)(2,1)}, u32[]{:S(2)}) %copy-start) | copy-done | bytes 4325400
  24.4 8.2 %middle_attention.1 = bf16[512,704]{1,0:T(8,128)(2,1)S(1)} custom-call(s32[1,1024]{1,0:T(1,128)S(1)} %copy-done.2, bf16[3,1024,704]{2,1,0:T(8,128)(2,1)S(1)} %copy-done, s32[8,128]{1,0:T(8,128)S(1)} %bitcast.27, s32[1024,1]{1,0:T(8,128)S(1)} %copy.38.refs_4_.refs_3_), custom_call_target="tpu_custom_call" | custom-call | flops 1107296256 | bytes 4325376 | tf_op jit(solution)/shard_map/middle_attention/pallas_call | solution.py:168
  32.6 1.7 %reshape.77 = bf16[128,2816]{1,0:T(8,128)(2,1)} reshape(bf16[512,704]{1,0:T(8,128)(2,1)S(1)} %middle_attention.1) | data formatting | bytes 1441792 | tf_op jit(solution)/shard_map/reshape | solution.py:239
  34.3 5.6 %fusion.12 = f32[128,1408]{1,0:T(8,128)} fusion(bf16[128,2816]{1,0:T(8,128)(2,1)} %reshape.77, bf16[2816,1408]{1,0:T(8,128)(2,1)} %bitcast.29), kind=kOutput, calls=%fused_computation.23 | convolution fusion | flops 1015021568 | bytes 9371648 | tf_op jit(solution)/shard_map/dot_general | solution.py:238
  40.0 15.0 %collective-permute-done.refs_5_ = bf16[2,272,704]{2,1,0:T(8,128)(2,1)S(1)} collective-permute-done((bf16[2,272,704]{2,1,0:T(8,128)(2,1)}, bf16[2,272,704]{2,1,0:T(8,128)(2,1)S(1)}, u32[]{:S(2)}, u32[]{:S(2)}) %collective-permute-start) | collective-permute-done | bytes 765984 | tf_op jit(solution)/shard_map/ppermute | solution.py:23
  55.0 0.5 slice.35
  56.2 0.7 collective-permute-done.1.refs_6_
  56.8 0.5 slice.37
  58.0 0.1 pad_add_fusion.refs_1_
  58.1 0.0 copy-start.1
  58.1 2.3 %copy-done.1 = bf16[3,1024,704]{2,1,0:T(8,128)(2,1)S(1)} copy-done((bf16[3,1024,704]{2,1,0:T(8,128)(2,1)S(1)}, bf16[3,1024,704]{2,1,0:T(8,128)(2,1)}, u32[]{:S(2)}) %copy-start.1) | copy-done | bytes 4325400
  60.4 11.8 %edge_attention.1 = bf16[512,704]{1,0:T(8,128)(2,1)S(1)} custom-call(s32[1,1024]{1,0:T(1,128)S(1)} %copy-done.2, s32[2]{0:T(128)S(1)} %pad_add_fusion.refs_1_, bf16[3,1024,704]{2,1,0:T(8,128)(2,1)S(1)} %copy-done.1, s32[8,128]{1,0:T(8,128)S(1)} %bitcast.28, s32[1024,1]{1,0:T(8,128)S(1)} %copy.38.refs_4_.refs_3_, ...), custom_call_target="tpu_custom_call" | custom-call | flops 1107296256 | bytes 4325376 | tf_op jit(solution)/shard_map/edge_attention/pallas_call | solution.py:168
  72.2 0.8 reshape.75
  73.1 0.0 copy-start.3
  73.1 4.6 %fusion.11 = f32[128,1408]{1,0:T(8,128)S(1)} fusion(bf16[128,2816]{1,0:T(8,128)(2,1)S(1)} %reshape.75, bf16[2816,1408]{1,0:T(8,128)(2,1)} %bitcast.30), kind=kOutput, calls=%fused_computation.22 | convolution fusion | flops 1015021568 | bytes 9371648 | tf_op jit(solution)/shard_map/dot_general | solution.py:238
  77.7 0.0 copy-start.6
  77.7 0.0 copy-start.4
  77.7 0.0 copy-start.5
  77.8 0.0 copy-done.3
  77.8 0.1 pad_maximum_fusion.mine_ref
  77.9 0.1 collective-permute-start.2
  78.0 0.4 copy-done.6
  78.3 0.2 convert_reduce_fusion
  78.5 0.1 iota_add_fusion
  78.6 0.1 add.35.target_ref
  78.7 0.0 copy-done.4
  78.7 0.0 copy-done.5
  78.7 2.5 %collective-permute-done.2.other_ref = f32[256,1408]{1,0:T(8,128)S(1)} collective-permute-done((f32[256,1408]{1,0:T(8,128)S(1)}, f32[256,1408]{1,0:T(8,128)S(1)}, u32[]{:S(2)}, u32[]{:S(2)}) %collective-permute-start.2) | collective-permute-done | bytes 1441824 | tf_op jit(solution)/shard_map/ppermute | solution.py:27
  81.2 1.2 norm_pack.1
  82.4 30.6 %all_to_all.5 = bf16[16,32,704]{2,1,0:T(8,128)(2,1)S(1)} all-to-all(bf16[16,32,704]{2,1,0:T(8,128)(2,1)S(1)} %bitcast.25), channel_id=1, replica_groups=mesh['grp'=16,'tp'=2] {'grp'}, dimensions={0} | all-to-all | bytes 1441792 | tf_op jit(solution)/shard_map/all_to_all | solution.py:271
  113.0 0.3 copy.41
  113.3 0.1 collective-permute-start.3
  113.4 2.2 %collective-permute-done.3 = bf16[512,704]{0,1:T(8,128)(2,1)S(1)} collective-permute-done((bf16[512,704]{0,1:T(8,128)(2,1)S(1)}, bf16[512,704]{0,1:T(8,128)(2,1)S(1)}, u32[]{:S(2)}, u32[]{:S(2)}) %collective-permute-start.3) | collective-permute-done | bytes 720928 | tf_op jit(solution)/shard_map/ppermute | solution.py:27
  115.5 0.3 copy.42
  115.8 0.2 broadcast_select_fusion.1
  116.0 7.6 %fusion = bf16[1,512,2112]{1,2,0:T(8,128)(2,1)} fusion(bf16[1408,2112]{0,1:T(8,128)(2,1)} %param.15, bf16[512,704]{1,0:T(8,128)(2,1)S(1)} %get-tuple-element.10, bf16[512,704]{1,0:T(8,128)(2,1)S(1)} %get-tuple-element.9), kind=kOutput, calls=%fused_computation.1 | convolution fusion | flops 3049029632 | bytes 9551872 | tf_op jit(solution)/shard_map/dot_general | solution.py:288
  (4 shorter events, 0.1 us)
Async XLA Ops:
  11.6 10.2 %copy-start.2 = (s32[1,1024]{1,0:T(1,128)S(1)}, s32[1,1024]{1,0:T(1,128)}, u32[]{:S(2)}) copy-start(s32[1,1024]{1,0:T(1,128)} %refs_0_.3) | copy-start | bytes 12292
  14.1 40.9 %collective-permute-start = (bf16[2,272,704]{2,1,0:T(8,128)(2,1)}, bf16[2,272,704]{2,1,0:T(8,128)(2,1)S(1)}, u32[]{:S(2)}, u32[]{:S(2)}) collective-permute-start(bf16[2,272,704]{2,1,0:T(8,128)(2,1)} %concatenate.12), channel_id=1, source_target_pairs={{0,2},{2,4},{4,6},{6,8},{8,10},{10,12},{12,14},{14,16},{16,18},{18... | collective-permute-start | bytes 2297864 | tf_op jit(solution)/shard_map/ppermute | solution.py:23
  20.5 36.3 %collective-permute-start.1 = (bf16[2,272,704]{2,1,0:T(8,128)(2,1)}, bf16[2,272,704]{2,1,0:T(8,128)(2,1)S(1)}, u32[]{:S(2)}, u32[]{:S(2)}) collective-permute-start(bf16[2,272,704]{2,1,0:T(8,128)(2,1)} %concatenate.13), channel_id=1, source_target_pairs={{2,0},{4,2},{6,4},{8,6},{10,8},{12,10},{14,12},{16,14},{18,16},{20... | collective-permute-start | bytes 2297864 | tf_op jit(solution)/shard_map/ppermute | solution.py:23
  22.1 2.3 %copy-start = (bf16[3,1024,704]{2,1,0:T(8,128)(2,1)S(1)}, bf16[3,1024,704]{2,1,0:T(8,128)(2,1)}, u32[]{:S(2)}) copy-start(bf16[3,1024,704]{2,1,0:T(8,128)(2,1)} %copy.35.refs_2_.refs_1_) | copy-start | bytes 12976132
  58.1 2.3 %copy-start.1 = (bf16[3,1024,704]{2,1,0:T(8,128)(2,1)S(1)}, bf16[3,1024,704]{2,1,0:T(8,128)(2,1)}, u32[]{:S(2)}) copy-start(bf16[3,1024,704]{2,1,0:T(8,128)(2,1)} %copy.35.refs_2_.refs_1_) | copy-start | bytes 12976132
  73.1 4.7 %copy-start.3 = (f32[128,1408]{1,0:T(8,128)S(1)}, f32[128,1408]{1,0:T(8,128)}, u32[]{:S(2)}) copy-start(f32[128,1408]{1,0:T(8,128)} %fusion.12) | copy-start | bytes 2162692
  77.7 0.7 copy-start.6
  77.7 1.0 copy-start.4
  77.7 1.0 copy-start.5
  77.9 3.3 %collective-permute-start.2 = (f32[256,1408]{1,0:T(8,128)S(1)}, f32[256,1408]{1,0:T(8,128)S(1)}, u32[]{:S(2)}, u32[]{:S(2)}) collective-permute-start(f32[256,1408]{1,0:T(8,128)S(1)} %pad_maximum_fusion.mine_ref), channel_id=1, source_target_pairs={{0,1},{1,0},{2,3},{3,2},{4,5},{5,4},{6,7},{7,6},{8,9},{9,8},{10,11... | collective-permute-start | bytes 4325384 | tf_op jit(solution)/shard_map/ppermute | solution.py:27
  113.3 2.3 %collective-permute-start.3 = (bf16[512,704]{0,1:T(8,128)(2,1)S(1)}, bf16[512,704]{0,1:T(8,128)(2,1)S(1)}, u32[]{:S(2)}, u32[]{:S(2)}) collective-permute-start(bf16[512,704]{0,1:T(8,128)(2,1)S(1)} %copy.41), channel_id=1, source_target_pairs={{0,1},{1,0},{2,3},{3,2},{4,5},{5,4},{6,7},{7,6},{8,9},{9,8},{10,11... | collective-permute-start | bytes 2162696 | tf_op jit(solution)/shard_map/ppermute | solution.py:27

commit v2 on v1

v2 whole, which is shorter than its diff:
```python
import functools
import math

import jax
import jax.numpy as jnp
from jax import lax
from jax.experimental import pallas as pl
from jax.experimental.pallas import tpu as pltpu
from jax.sharding import PartitionSpec as P

DH = 88
WIN = 4
CAP = 2
TILE = 128
PACK = 16
EPS = 1e-05
NEG = -1e30
SCALE2 = math.log2(math.e) / math.sqrt(DH)


def shifted(block, axis, distance):
    devices = range(lax.axis_size(axis))
    route = [(i - distance, i) for i in devices if i - distance in devices]
    return lax.ppermute(block, axis, route)


def swapped(block, axis):
    return lax.ppermute(block, axis, [(0, 1), (1, 0)])


def head_scores(query, keys, bias):
    scores = lax.dot_general(keys, query, (((0,), (0,)), ((), ())), preferred_element_type=jnp.float32)
    return scores * SCALE2 + bias


def attend_heads(width, read_query, key_parts, bias_parts, value_parts):
    pieces = []
    for head in range(width // DH):
        low = head * DH
        start = low // PACK * PACK
        stop = -(-(low + DH) // PACK) * PACK
        row = start + lax.broadcasted_iota(jnp.int32, (stop - start, 1), 0)
        inside = jnp.logical_and(row >= low, row < low + DH)
        query = read_query(start, stop)
        query = jnp.where(inside, query.astype(jnp.float32), 0.0).astype(jnp.bfloat16)
        scores = [head_scores(query, keys(start, stop), bias) for keys, bias in zip(key_parts, bias_parts)]
        top = jnp.max(scores[0], axis=0, keepdims=True)
        for part in scores[1:]:
            top = jnp.maximum(top, jnp.max(part, axis=0, keepdims=True))
        weights = [jnp.exp2(part - top) for part in scores]
        total = jnp.sum(weights[0], axis=0, keepdims=True)
        for part in weights[1:]:
            total = total + jnp.sum(part, axis=0, keepdims=True)
        scale = 1.0 / total
        mixed = None
        for part, values in zip(weights, value_parts):
            term = jnp.dot(
                values(start, stop), (part * scale).astype(jnp.bfloat16), preferred_element_type=jnp.float32
            )
            mixed = term if mixed is None else mixed + term
        pieces.append(mixed[low - start : low - start + DH])
    return jnp.concatenate(pieces, axis=0)


def attention_kernel(edge, row_len, width, sent, *refs):
    if edge:
        seg_smem, qkv, seg_row, seg_col, merge_hbm, links, prev, following, middle, out = refs[:10]
    else:
        seg_smem, qkv, seg_row, seg_col, merge_hbm, out = refs[:6]
    attended, merge_vmem, merge_sem = refs[-3:]
    tiles = row_len // TILE
    edge_tiles = sent // TILE
    tokens = TILE // WIN
    fetch = pltpu.make_async_copy(merge_hbm, merge_vmem, merge_sem)
    fetch.start()
    ordered = lax.broadcasted_iota(jnp.int32, (TILE, TILE), 0)
    ordered = (ordered % tokens) * WIN + ordered // tokens
    order = (ordered == lax.broadcasted_iota(jnp.int32, (TILE, TILE), 1)).astype(jnp.float32)
    order = order.astype(jnp.bfloat16)

    def one(tile, out_row, neighbour):
        first = seg_smem[0, tile * TILE]
        last = seg_smem[0, tile * TILE + TILE - 1]
        begin, stop = jnp.int32(0), jnp.int32(0)
        for other in range(tiles):
            begin += (seg_smem[0, other * TILE + TILE - 1] < first).astype(jnp.int32)
            stop += (seg_smem[0, other * TILE] <= last).astype(jnp.int32)
        needed = stop - begin
        query_at = pl.multiple_of(tile * TILE, TILE)
        query_ids = seg_row[pl.ds(tile, 1), :]

        def run(count):
            key_at = pl.multiple_of(jnp.minimum(begin, tiles - count) * TILE, TILE)
            key_ids = seg_col[pl.ds(key_at, count * TILE), :]
            bias_parts = [jnp.where(key_ids == query_ids, 0.0, NEG)]
            key_parts = [lambda a, b: qkv[1, a:b, pl.ds(key_at, count * TILE)]]
            value_parts = [lambda a, b: qkv[2, a:b, pl.ds(key_at, count * TILE)]]
            if neighbour is not None:
                source, segment, open_link = neighbour
                marks = jnp.transpose(source[0, width : width + PACK, :].astype(jnp.float32))[:, :1]
                wanted = jnp.logical_and(query_ids == segment, open_link).astype(jnp.float32)
                bias_parts.append(jnp.where(marks * wanted > 0.5, 0.0, NEG))
                key_parts.append(lambda a, b: source[0, a:b, :])
                value_parts.append(lambda a, b: source[1, a:b, :])
            mixed = attend_heads(
                width,
                lambda a, b: qkv[0, a:b, pl.ds(query_at, TILE)],
                key_parts,
                bias_parts,
                value_parts,
            )
            turned = lax.dot_general(
                order,
                mixed.astype(jnp.bfloat16),
                (((1,), (1,)), ((), ())),
                preferred_element_type=jnp.float32,
            ).astype(jnp.bfloat16)
            for j in range(WIN):
                attended[j, pl.ds(out_row, tokens), :] = turned[j * tokens : (j + 1) * tokens]

        sizes = [size for size in (2, 3, 4) if size < tiles] + [tiles]
        floor = 0
        for size in sizes:
            pl.when(jnp.logical_and(needed > floor, needed <= size))(functools.partial(run, size))
            floor = size

    if edge:
        @pl.loop(0, edge_tiles)
        def _(tile):
            one(tile, pl.multiple_of(tile * tokens, tokens), (prev, seg_smem[0, 0], True))

        @pl.loop(0, edge_tiles)
        def _(step):
            one(
                tiles - edge_tiles + step,
                pl.multiple_of((edge_tiles + step) * tokens, tokens),
                (following, seg_smem[0, row_len - 1], links[0] > 0),
            )
    else:
        @pl.loop(edge_tiles, tiles - edge_tiles)
        def _(tile):
            one(tile, pl.multiple_of((tile - edge_tiles) * tokens, tokens), None)

    fetch.wait()
    merged = jnp.dot(attended[0], merge_vmem[0], preferred_element_type=jnp.float32)
    for j in range(1, WIN):
        merged += jnp.dot(attended[j], merge_vmem[j], preferred_element_type=jnp.float32)
    if edge:
        half = merged.shape[0] // 2
        out[:half, :] = merged[:half]
        out[half : half + middle.shape[0], :] = middle[...]
        out[half + middle.shape[0] :, :] = merged[half:]
    else:
        out[...] = merged


def run_attention(edge, qkv, segments, merge_weight, sent, extra):
    width, row_len = qkv.shape[1:]
    model_width = merge_weight.shape[2]
    rows = 2 * sent if edge else row_len - 2 * sent
    smem = pl.BlockSpec(memory_space=pltpu.SMEM)
    vmem = pl.BlockSpec(memory_space=pltpu.VMEM)
    operands = [
        segments,
        qkv,
        segments.reshape(row_len // TILE, TILE),
        segments.reshape(row_len, 1),
        merge_weight,
    ]
    specs = [smem, vmem, vmem, vmem, pl.BlockSpec(memory_space=pl.ANY)]
    if edge:
        operands += list(extra)
        specs += [smem, vmem, vmem, vmem]
    out_rows = row_len // WIN if edge else rows // WIN
    return pl.pallas_call(
        functools.partial(attention_kernel, edge, row_len, width, sent),
        out_shape=jax.ShapeDtypeStruct((out_rows, model_width), jnp.float32),
        in_specs=specs,
        out_specs=vmem,
        scratch_shapes=[
            pltpu.VMEM((WIN, rows // WIN, width), jnp.bfloat16),
            pltpu.VMEM(merge_weight.shape, jnp.bfloat16),
            pltpu.SemaphoreType.DMA,
        ],
        compiler_params=pltpu.CompilerParams(vmem_limit_bytes=28 << 20),
        cost_estimate=pl.CostEstimate(
            flops=rows * 512 * width * 6, bytes_accessed=qkv.size * 2, transcendentals=rows * 512 * 8
        ),
        name="edge_attention" if edge else "middle_attention",
    )(*operands)


def norm_pack_kernel(width, mine_ref, other_ref, gain_ref, bias_ref, target_ref, half_ref, out_ref):
    merged = mine_ref[...] + other_ref[...]
    model_width = merged.shape[1]
    mean = jnp.sum(merged, axis=1, keepdims=True) / model_width
    variance = jnp.sum(merged * merged, axis=1, keepdims=True) / model_width - mean * mean
    normed = (merged - mean) * lax.rsqrt(variance + EPS) * gain_ref[...] + bias_ref[...]
    normed = normed.astype(jnp.bfloat16)
    left, right = normed[:, :width], normed[:, model_width - width :]
    place = lax.broadcasted_iota(jnp.int32, (out_ref.shape[0], merged.shape[0]), 0)
    place = jnp.where(place == target_ref[...], 1.0, 0.0).astype(jnp.bfloat16)
    half = half_ref[0]

    @pl.when(half == 0)
    def _():
        out_ref[...] = jnp.dot(place, left, preferred_element_type=jnp.float32).astype(jnp.bfloat16)

    @pl.when(half != 0)
    def _():
        out_ref[...] = jnp.dot(place, right, preferred_element_type=jnp.float32).astype(jnp.bfloat16)


def norm_pack(mine, other, gain, bias, target, half, slots, width):
    vmem = pl.BlockSpec(memory_space=pltpu.VMEM)
    return pl.pallas_call(
        functools.partial(norm_pack_kernel, width),
        out_shape=jax.ShapeDtypeStruct((slots, width), jnp.bfloat16),
        in_specs=[vmem] * 5 + [pl.BlockSpec(memory_space=pltpu.SMEM)],
        out_specs=vmem,
        compiler_params=pltpu.CompilerParams(vmem_limit_bytes=32 << 20),
        name="norm_pack",
    )(mine, other, gain[None], bias[None], target[None], half)


def project_kernel(half_ref, mine_ref, other_ref, weight_ref, out_ref, routed):
    width, model_width = mine_ref.shape[1], routed.shape[1]

    def place(left, right):
        routed[:, :width] = left[...]
        routed[:, model_width - width :] = right[...]

    first = pl.program_id(0) == 0
    pl.when(jnp.logical_and(first, half_ref[0] == 0))(lambda: place(mine_ref, other_ref))
    pl.when(jnp.logical_and(first, half_ref[0] != 0))(lambda: place(other_ref, mine_ref))
    out_ref[...] = lax.dot_general(
        weight_ref[...], routed[...], (((1,), (1,)), ((), ())), preferred_element_type=jnp.float32
    ).astype(jnp.bfloat16)


def project(half, mine, other, weight):
    columns, model_width = weight.shape
    slots, width = mine.shape
    step = next(s for s in (352, 264, 176, 128, 64, 32, 16, columns) if columns % s == 0)
    return pl.pallas_call(
        project_kernel,
        grid=(columns // step,),
        out_shape=jax.ShapeDtypeStruct((columns, slots), jnp.bfloat16),
        in_specs=[
            pl.BlockSpec(memory_space=pltpu.SMEM),
            pl.BlockSpec((slots, width), lambda i: (0, 0)),
            pl.BlockSpec((slots, width), lambda i: (0, 0)),
            pl.BlockSpec((step, model_width), lambda i: (i, 0)),
        ],
        out_specs=pl.BlockSpec((step, slots), lambda i: (i, 0)),
        scratch_shapes=[pltpu.VMEM((slots, model_width), jnp.bfloat16)],
        compiler_params=pltpu.CompilerParams(vmem_limit_bytes=32 << 20),
        name="project",
    )(half, mine, other, weight)


def body(qkv, segments, links, owners, merge_weight, norm_gain, norm_bias, next_weight):
    row_len = qkv.shape[1]
    model_width = norm_gain.shape[0]
    tp_size = lax.axis_size("tp")
    seg_ids = segments[0]
    linked = links[0] > 0
    sent = row_len // 4
    turned = jnp.swapaxes(qkv, 1, 2)
    last_flag = jnp.logical_and(seg_ids == seg_ids[row_len - 1], linked)[row_len - sent :]
    first_flag = (seg_ids == seg_ids[0])[:sent]

    def payload(pairs, flag):
        mark = jnp.broadcast_to(flag.astype(jnp.bfloat16)[None, None, :], (2, PACK, sent))
        return jnp.concatenate([pairs, mark], axis=1)

    prev = shifted(payload(turned[1:3, :, row_len - sent :], last_flag), "grp", 1)
    following = shifted(payload(turned[1:3, :, :sent], first_flag), "grp", -1)
    middle = run_attention(False, turned, segments, merge_weight, sent, None)
    partial_sum = run_attention(
        True, turned, segments, merge_weight, sent, (links, prev, following, middle)
    )
    merged_rows = row_len // WIN

    owner_ids = owners[0, :, 0]
    block_count = owner_ids.shape[0]
    group_count = lax.axis_size("grp")
    block_rows = merged_rows // block_count
    block_index = jnp.arange(block_count)
    earlier = block_index[:, None] > block_index[None, :]
    slot_rank = jnp.sum(
        jnp.logical_and(owner_ids[:, None] == owner_ids[None, :], earlier).astype(jnp.int32), axis=1
    )
    target = (owner_ids * CAP + slot_rank)[:, None] * block_rows + jnp.arange(block_rows)[None, :]
    target = target.reshape(merged_rows)
    slots = group_count * CAP * block_rows

    if tp_size == 2:
        half_index = lax.axis_index("tp")[None].astype(jnp.int32)
        other = swapped(partial_sum, "tp")
        part_width = -(-(model_width // 2) // TILE) * TILE
        packed = norm_pack(
            partial_sum, other, norm_gain, norm_bias, target, half_index, slots, part_width
        )
        packed = packed.reshape(group_count, CAP * block_rows, part_width)
        arrived = lax.all_to_all(packed, "grp", split_axis=0, concat_axis=0, tiled=True)
        arrived = arrived.reshape(slots, part_width)
        beside = swapped(arrived, "tp")
        projected = project(half_index, arrived, beside, next_weight.T)
        return projected.T[None]
    else:
        merged = lax.psum(partial_sum, "tp")
        mean = jnp.mean(merged, axis=1, keepdims=True)
        variance = jnp.mean(merged * merged, axis=1, keepdims=True) - mean * mean
        normed = (merged - mean) * lax.rsqrt(variance + EPS) * norm_gain + norm_bias
        normed = normed.astype(jnp.bfloat16)
        placing = (jnp.arange(slots)[:, None] == target[None, :]).astype(jnp.bfloat16)
        packed = jnp.dot(placing, normed, preferred_element_type=jnp.float32).astype(jnp.bfloat16)
        packed = packed.reshape(group_count, CAP * block_rows, model_width)
        routed = lax.all_to_all(packed, "grp", split_axis=0, concat_axis=0, tiled=True)
        routed = routed.reshape(slots, model_width)
    projected = jnp.dot(routed, next_weight, preferred_element_type=jnp.float32)
    return projected.astype(jnp.bfloat16)[None]


def solution(mesh):
    placed = (
        P(None, "grp", "tp"),
        P("grp", None),
        P("grp"),
        P("grp", None, None),
        P(None, "tp", None),
        P(),
        P(),
        P(None, "tp"),
    )
    return jax.shard_map(
        body, mesh=mesh, in_specs=placed, out_specs=P("grp", None, "tp"), check_vma=False
    )
```

time: 123 us -> 103 us (0.84); the launches traced: 124 us -> 101 us
  matrix products: 17.9 us -> 0 us
  Pallas kernels: 21.3 us -> 33.8 us
  local copies, waits for them, and re-layouts: 20.7 us -> 11.3 us
  between operations: 3.38 us -> 0.82 us
  waiting for transfers between devices: 20.3 us -> 17.8 us
  blocking collectives: 30.6 us -> 28.9 us
    dot_general x3 -> x0, matrix products: 17.9 us -> none  [the longest x2 10.3 us: merge(): jnp.dot(attended.reshape(-1, WIN * shard_width), merge_flat, preferred_el...]
    pallas_call x2, Pallas kernels: 20 us -> 27.3 us  [run_attention(): pl.pallas_call(functools.partial(attention_kernel, edge, row_len, width,...]
    pallas_call x0 -> x1, Pallas kernels: none -> 5.52 us  [project(): pl.pallas_call(project_kernel, grid=(columns // step,), out_shape=jax.Sha...]
    unnamed x15 -> x14, local copies, waits for them, and re-layouts: 11.6 us -> 8.18 us
    ppermute x2, waiting for transfers between devices: 15.7 us -> 12.7 us  [shifted(): return lax.ppermute(block, axis, route)]
    reshape x3 -> x0, local copies, waits for them, and re-layouts: 2.76 us -> none  [the longest x2 2.5 us: merge(): attended.reshape(-1, WIN * shard_width)]
    reduce_sum x1 -> x0, other arithmetic: 2.55 us -> none  [body(): last_count = jnp.sum((seg_ids == seg_ids[row_len - 1]).astype(jnp.int32))]
    concatenate x2 -> x0, local copies, waits for them, and re-layouts: 1.97 us -> none  [payload(): return jnp.concatenate([pairs, mark], axis=1)]
  transfers between devices with their start and end apart: 4 -> 4, of which waited for: 4 -> 4; matrix products, arithmetic and copies ran while one was open for 8% -> 1% of each run, Pallas kernels for 7% -> 13%
where the time goes in v2:
time: 103 us; the launch traced here: 101 us
  Pallas kernels  33.8 us (33%)
  blocking collectives  28.9 us (28%)
  waiting for transfers between devices  17.8 us (17%)
  local copies, waits for them, and re-layouts  11.3 us (11%)
  starting transfers between devices  6.24 us (6%)
  other arithmetic  2.45 us (2%)
    all_to_all x1, blocking collectives, body(): lax.all_to_all(packed, 'grp', split_axis=0, concat_axis=0, tiled=True)  28.9 us
    pallas_call x2, Pallas kernels, run_attention(): pl.pallas_call(functools.partial(attention_kernel, edge, row_len, width,...  27.3 us
    ppermute x2, waiting for transfers between devices, shifted(): return lax.ppermute(block, axis, route)  12.7 us
    unnamed x14, local copies, waits for them, and re-layouts  8.18 us
    ppermute x2, starting transfers between devices, shifted(): return lax.ppermute(block, axis, route)  6.17 us
    pallas_call x1, Pallas kernels, project(): pl.pallas_call(project_kernel, grid=(columns // step,), out_shape=jax.Sha...  5.52 us
    ppermute x2, waiting for transfers between devices, swapped(): return lax.ppermute(block, axis, [(0, 1), (1, 0)])  5.09 us
  transfers between devices with their start and end apart: 4, of which 4 were waited for; matrix products, arithmetic and copies ran while one was open for 1% of the time, Pallas kernels for 13%

profile of v2, /device:TPU:0, one launch (start us, length us, event | category | flops | bytes accessed | tf_op | source)
XLA Modules:
  0.0 101.4 jit_solution(3307326824798489880)
XLA Ops:
  0.0 0.0 copy-start.3
  0.0 1.3 %fusion.4 = (s32[1,1]{1,0:T(1,128)}, s32[1,1]{1,0:T(1,128)}) fusion(s32[1,1024]{1,0:T(1,128)} %refs_0_.3), kind=kLoop, calls=%fused_computation.12 | loop fusion | bytes 16 | tf_op jit(solution)/shard_map/slice | solution.py:270
  2.0 1.4 %fusion.3 = (bf16[2,704,256]{2,1,0:T(8,128)(2,1)S(1)}, bf16[2,704,256]{2,1,0:T(8,128)(2,1)S(1)}) fusion(bf16[3,704,1024]{2,1,0:T(8,128)(2,1)} %bitcast.15), kind=kLoop, calls=%fused_computation.11 | loop fusion | bytes 2883584 | tf_op jit(solution)/shard_map/slice | solution.py:278
  3.4 0.0 copy-done.3
  3.4 1.2 %fusion.1 = (bf16[256]{0:T(256)(128)(2,1)S(1)}, bf16[256]{0:T(256)(128)(2,1)S(1)}) fusion(s32[1,1024]{1,0:T(1,128)S(1)} %copy-done.3, s32[]{:T(128)} %bitcast.6, pred[]{:T(512)} %bitcast.5, s32[]{:T(128)} %bitcast.4), kind=kLoop, calls=%fused_computation.8 | loop fusion | flops 1280 | bytes 3081 | tf_op jit(solution)/shard_map/convert_element_type | solution.py:274
  4.7 0.1 pad_maximum_fusion
  4.7 4.9 %collective-permute-start = (bf16[2,720,256]{2,1,0:T(8,128)(2,1)S(1)}, bf16[2,720,256]{2,1,0:T(8,128)(2,1)S(1)}, u32[]{:S(2)}, u32[]{:S(2)}) collective-permute-start(bf16[2,720,256]{2,1,0:T(8,128)(2,1)S(1)} %pad_maximum_fusion), channel_id=1, source_target_pairs={{0,2},{2,4},{4,6},{6,8},{8,10},{10,12},{12,14},{14,16},{16,18},{18... | collective-permute-start | bytes 2211848 | tf_op jit(solution)/shard_map/ppermute | solution.py:24
  9.6 0.9 pad_maximum_fusion.1
  10.5 1.3 %collective-permute-start.1 = (bf16[2,720,256]{2,1,0:T(8,128)(2,1)}, bf16[2,720,256]{2,1,0:T(8,128)(2,1)S(1)}, u32[]{:S(2)}, u32[]{:S(2)}) collective-permute-start(bf16[2,720,256]{2,1,0:T(8,128)(2,1)} %pad_maximum_fusion.1), channel_id=1, source_target_pairs={{2,0},{4,2},{6,4},{8,6},{10,8},{12,10},{14,12},{16,14},{18,16},{20... | collective-permute-start | bytes 2211848 | tf_op jit(solution)/shard_map/ppermute | solution.py:24
  11.8 0.2 copy.12.refs_3_
  12.1 0.0 copy-start
  12.1 3.2 %copy-done = bf16[4,704,1408]{2,1,0:T(8,128)(2,1)S(1)} copy-done((bf16[4,704,1408]{2,1,0:T(8,128)(2,1)S(1)}, bf16[4,704,1408]{2,1,0:T(8,128)(2,1)}, u32[]{:S(2)}) %copy-start) | copy-done | bytes 7929880
  15.3 0.0 copy-start.1
  15.3 2.2 %copy-done.1 = bf16[3,1024,704]{1,2,0:T(8,128)(2,1)S(1)} copy-done((bf16[3,1024,704]{1,2,0:T(8,128)(2,1)S(1)}, bf16[3,1024,704]{1,2,0:T(8,128)(2,1)}, u32[]{:S(2)}) %copy-start.1) | copy-done | bytes 4325400
  17.5 12.7 %middle_attention.1.refs_8_ = f32[128,1408]{1,0:T(8,128)S(1)} custom-call(s32[1,1024]{1,0:T(1,128)S(1)} %copy-done.3, bf16[3,704,1024]{2,1,0:T(8,128)(2,1)S(1)} %bitcast.16, s32[8,128]{1,0:T(8,128)S(1)} %bitcast.23, s32[1024,1]{1,0:T(8,128)S(1)} %copy.12.refs_3_, bf16[4,704,1408]{2,1,0:T(8,128)(2,1)S(1)} %copy-done), custom_call_target="tpu_custom_call" | custom-call | flops 1107296256 | bytes 4325376 | tf_op jit(solution)/shard_map/middle_attention/pallas_call | solution.py:175
  30.3 0.0 copy-start.6
  30.3 0.0 copy-start.4
  30.3 0.0 copy-start.5
  30.3 10.8 %collective-permute-done.refs_6_ = bf16[2,720,256]{2,1,0:T(8,128)(2,1)S(1)} collective-permute-done((bf16[2,720,256]{2,1,0:T(8,128)(2,1)S(1)}, bf16[2,720,256]{2,1,0:T(8,128)(2,1)S(1)}, u32[]{:S(2)}, u32[]{:S(2)}) %collective-permute-start) | collective-permute-done | bytes 737312 | tf_op jit(solution)/shard_map/ppermute | solution.py:24
  41.1 1.9 %collective-permute-done.1.refs_7_ = bf16[2,720,256]{2,1,0:T(8,128)(2,1)S(1)} collective-permute-done((bf16[2,720,256]{2,1,0:T(8,128)(2,1)}, bf16[2,720,256]{2,1,0:T(8,128)(2,1)S(1)}, u32[]{:S(2)}, u32[]{:S(2)}) %collective-permute-start.1) | collective-permute-done | bytes 737312 | tf_op jit(solution)/shard_map/ppermute | solution.py:24
  43.0 14.6 %edge_attention.1.mine_ref = f32[256,1408]{1,0:T(8,128)S(1)} custom-call(s32[1,1024]{1,0:T(1,128)S(1)} %copy-done.3, bf16[3,704,1024]{2,1,0:T(8,128)(2,1)S(1)} %bitcast.17, s32[8,128]{1,0:T(8,128)S(1)} %bitcast.24, s32[1024,1]{1,0:T(8,128)S(1)} %copy.12.refs_3_, bf16[4,704,1408]{2,1,0:T(8,128)(2,1)S(1)} %copy-done, s32[1]{0:T(128)S(6)} %copy.13.refs_5_, ...), custom_call_target="tpu_custom_call" | custom-call | flops 1107296256 | bytes 4325376 | tf_op jit(solution)/shard_map/edge_attention/pallas_call | solution.py:175
  57.6 0.1 collective-permute-start.2
  57.7 0.0 copy-done.6
  57.7 0.2 convert_reduce_fusion
  57.9 0.1 iota_add_fusion
  58.0 0.1 add.31.target_ref
  58.1 0.0 copy-done.4
  58.1 0.0 copy-done.5
  58.1 2.8 %collective-permute-done.2.other_ref = f32[256,1408]{1,0:T(8,128)S(1)} collective-permute-done((f32[256,1408]{1,0:T(8,128)S(1)}, f32[256,1408]{1,0:T(8,128)S(1)}, u32[]{:S(2)}, u32[]{:S(2)}) %collective-permute-start.2) | collective-permute-done | bytes 1441824 | tf_op jit(solution)/shard_map/ppermute | solution.py:28
  60.9 1.0 norm_pack.1
  61.9 28.9 %all_to_all.5 = bf16[16,32,768]{2,1,0:T(8,128)(2,1)S(1)} all-to-all(bf16[16,32,768]{2,1,0:T(8,128)(2,1)S(1)} %bitcast.21), channel_id=1, replica_groups=mesh['grp'=16,'tp'=2] {'grp'}, dimensions={0} | all-to-all | bytes 1572864 | tf_op jit(solution)/shard_map/all_to_all | solution.py:306
  90.9 0.0 collective-permute-start.3
  90.9 2.3 %collective-permute-done.3.other_ref = bf16[512,768]{1,0:T(8,128)(2,1)S(1)} collective-permute-done((bf16[512,768]{1,0:T(8,128)(2,1)S(1)}, bf16[512,768]{1,0:T(8,128)(2,1)S(1)}, u32[]{:S(2)}, u32[]{:S(2)}) %collective-permute-start.3) | collective-permute-done | bytes 786464 | tf_op jit(solution)/shard_map/ppermute | solution.py:28
  93.1 0.0 copy-start.2
  93.1 2.7 %copy-done.2 = bf16[1408,2112]{0,1:T(8,128)(2,1)S(1)} copy-done((bf16[1408,2112]{0,1:T(8,128)(2,1)S(1)}, bf16[1408,2112]{0,1:T(8,128)(2,1)}, u32[]{:S(2)}) %copy-start.2) | copy-done | bytes 5947416
  95.8 5.5 %project.1 = bf16[2112,512]{1,0:T(8,128)(2,1)} custom-call(s32[1]{0:T(128)} %bitcast.half_ref, bf16[512,768]{1,0:T(8,128)(2,1)S(1)} %bitcast.20, bf16[512,768]{1,0:T(8,128)(2,1)S(1)} %collective-permute-done.3.other_ref, bf16[2112,1408]{1,0:T(8,128)(2,1)S(1)} %bitcast.18), custom_call_target="tpu_custom_call" | custom-call | tf_op jit(solution)/shard_map/project/pallas_call | solution.py:245
  (5 shorter events, 0.0 us)
Async XLA Ops:
  0.0 3.4 %copy-start.3 = (s32[1,1024]{1,0:T(1,128)S(1)}, s32[1,1024]{1,0:T(1,128)}, u32[]{:S(2)}) copy-start(s32[1,1024]{1,0:T(1,128)} %refs_0_.3) | copy-start | bytes 12292
  4.7 36.4 %collective-permute-start = (bf16[2,720,256]{2,1,0:T(8,128)(2,1)S(1)}, bf16[2,720,256]{2,1,0:T(8,128)(2,1)S(1)}, u32[]{:S(2)}, u32[]{:S(2)}) collective-permute-start(bf16[2,720,256]{2,1,0:T(8,128)(2,1)S(1)} %pad_maximum_fusion), channel_id=1, source_target_pairs={{0,2},{2,4},{4,6},{6,8},{8,10},{10,12},{12,14},{14,16},{16,18},{18... | collective-permute-start | bytes 2211848 | tf_op jit(solution)/shard_map/ppermute | solution.py:24
  10.5 32.5 %collective-permute-start.1 = (bf16[2,720,256]{2,1,0:T(8,128)(2,1)}, bf16[2,720,256]{2,1,0:T(8,128)(2,1)S(1)}, u32[]{:S(2)}, u32[]{:S(2)}) collective-permute-start(bf16[2,720,256]{2,1,0:T(8,128)(2,1)} %pad_maximum_fusion.1), channel_id=1, source_target_pairs={{2,0},{4,2},{6,4},{8,6},{10,8},{12,10},{14,12},{16,14},{18,16},{20... | collective-permute-start | bytes 2211848 | tf_op jit(solution)/shard_map/ppermute | solution.py:24
  12.1 3.3 %copy-start = (bf16[4,704,1408]{2,1,0:T(8,128)(2,1)S(1)}, bf16[4,704,1408]{2,1,0:T(8,128)(2,1)}, u32[]{:S(2)}) copy-start(bf16[4,704,1408]{2,1,0:T(8,128)(2,1)} %refs_4_.3) | copy-start | bytes 23789572
  15.3 2.2 %copy-start.1 = (bf16[3,1024,704]{1,2,0:T(8,128)(2,1)S(1)}, bf16[3,1024,704]{1,2,0:T(8,128)(2,1)}, u32[]{:S(2)}) copy-start(bf16[3,1024,704]{1,2,0:T(8,128)(2,1)} %param.8) | copy-start | bytes 12976132
  30.3 27.5 %copy-start.6 = (s32[1,16,1]{1,2,0:T(1,128)S(1)}, s32[1,16,1]{1,2,0:T(1,128)}, u32[]{:S(2)}) copy-start(s32[1,16,1]{1,2,0:T(1,128)} %param.11) | copy-start | bytes 196
  30.3 27.8 %copy-start.4 = (f32[1408]{0:T(1024)S(1)}, f32[1408]{0:T(1024)}, u32[]{:S(2)}) copy-start(f32[1408]{0:T(1024)} %param.13) | copy-start | bytes 16900
  30.3 27.8 %copy-start.5 = (f32[1408]{0:T(1024)S(1)}, f32[1408]{0:T(1024)}, u32[]{:S(2)}) copy-start(f32[1408]{0:T(1024)} %param.14) | copy-start | bytes 16900
  57.6 3.3 %collective-permute-start.2 = (f32[256,1408]{1,0:T(8,128)S(1)}, f32[256,1408]{1,0:T(8,128)S(1)}, u32[]{:S(2)}, u32[]{:S(2)}) collective-permute-start(f32[256,1408]{1,0:T(8,128)S(1)} %edge_attention.1.mine_ref), channel_id=1, source_target_pairs={{0,1},{1,0},{2,3},{3,2},{4,5},{5,4},{6,7},{7,6},{8,9},{9,8},{10,11... | collective-permute-start | bytes 4325384 | tf_op jit(solution)/shard_map/ppermute | solution.py:28
  90.9 2.3 %collective-permute-start.3 = (bf16[512,768]{1,0:T(8,128)(2,1)S(1)}, bf16[512,768]{1,0:T(8,128)(2,1)S(1)}, u32[]{:S(2)}, u32[]{:S(2)}) collective-permute-start(bf16[512,768]{1,0:T(8,128)(2,1)S(1)} %bitcast.19), channel_id=1, source_target_pairs={{0,1},{1,0},{2,3},{3,2},{4,5},{5,4},{6,7},{7,6},{8,9},{9,8},{10,11... | collective-permute-start | bytes 2359304 | tf_op jit(solution)/shard_map/ppermute | solution.py:28
  93.1 2.7 %copy-start.2 = (bf16[1408,2112]{0,1:T(8,128)(2,1)S(1)}, bf16[1408,2112]{0,1:T(8,128)(2,1)}, u32[]{:S(2)}) copy-start(bf16[1408,2112]{0,1:T(8,128)(2,1)} %param.15) | copy-start | bytes 17842180

commit v3 on v2

--- a/solution.py
+++ b/solution.py
@@ -28,51 +28,67 @@
     return lax.ppermute(block, axis, [(0, 1), (1, 0)])
 
 
-def head_scores(query, keys, bias):
-    scores = lax.dot_general(keys, query, (((0,), (0,)), ((), ())), preferred_element_type=jnp.float32)
-    return scores * SCALE2 + bias
-
-
-def attend_heads(width, read_query, key_parts, bias_parts, value_parts):
+def attend_heads(width, read_query, key_parts, bias_parts, value_parts, together=4):
     pieces = []
-    for head in range(width // DH):
-        low = head * DH
-        start = low // PACK * PACK
-        stop = -(-(low + DH) // PACK) * PACK
-        row = start + lax.broadcasted_iota(jnp.int32, (stop - start, 1), 0)
-        inside = jnp.logical_and(row >= low, row < low + DH)
-        query = read_query(start, stop)
-        query = jnp.where(inside, query.astype(jnp.float32), 0.0).astype(jnp.bfloat16)
-        scores = [head_scores(query, keys(start, stop), bias) for keys, bias in zip(key_parts, bias_parts)]
-        top = jnp.max(scores[0], axis=0, keepdims=True)
-        for part in scores[1:]:
-            top = jnp.maximum(top, jnp.max(part, axis=0, keepdims=True))
-        weights = [jnp.exp2(part - top) for part in scores]
-        total = jnp.sum(weights[0], axis=0, keepdims=True)
-        for part in weights[1:]:
-            total = total + jnp.sum(part, axis=0, keepdims=True)
-        scale = 1.0 / total
-        mixed = None
-        for part, values in zip(weights, value_parts):
-            term = jnp.dot(
-                values(start, stop), (part * scale).astype(jnp.bfloat16), preferred_element_type=jnp.float32
+    for base in range(0, width // DH, together):
+        lows = [head * DH for head in range(base, min(base + together, width // DH))]
+        scores = []
+        for low in lows:
+            start, stop = low // TILE * TILE, min(width, -(-(low + DH) // TILE) * TILE)
+            row = start + lax.broadcasted_iota(jnp.int32, (stop - start, 1), 0)
+            inside = jnp.logical_and(row >= low, row < low + DH)
+            query = read_query(start, stop)
+            query = jnp.where(inside, query.astype(jnp.float32), 0.0).astype(jnp.bfloat16)
+            scores.append(
+                [jnp.dot(keys(start, stop), query, preferred_element_type=jnp.float32) for keys in key_parts]
             )
-            mixed = term if mixed is None else mixed + term
-        pieces.append(mixed[low - start : low - start + DH])
+        scores = [[part * SCALE2 + bias for part, bias in zip(parts, bias_parts)] for parts in scores]
+        tops = [
+            functools.reduce(jnp.maximum, [jnp.max(part, axis=0, keepdims=True) for part in parts])
+            for parts in scores
+        ]
+        weights = [[jnp.exp2(part - top) for part in parts] for parts, top in zip(scores, tops)]
+        scales = [
+            1.0 / functools.reduce(jnp.add, [jnp.sum(part, axis=0, keepdims=True) for part in parts])
+            for parts in weights
+        ]
+        weights = [
+            [(part * scale).astype(jnp.bfloat16) for part in parts] for parts, scale in zip(weights, scales)
+        ]
+        for low, parts in zip(lows, weights):
+            start, stop = low // PACK * PACK, -(-(low + DH) // PACK) * PACK
+            terms = [
+                jnp.dot(values(start, stop), part, preferred_element_type=jnp.float32)
+                for part, values in zip(parts, value_parts)
+            ]
+            pieces.append(functools.reduce(jnp.add, terms)[low - start : low - start + DH])
     return jnp.concatenate(pieces, axis=0)
 
 
 def attention_kernel(edge, row_len, width, sent, *refs):
     if edge:
-        seg_smem, qkv, seg_row, seg_col, merge_hbm, links, prev, following, middle, out = refs[:10]
+        seg_smem, qkv_hbm, seg_row, seg_col, merge_hbm, links, prev, following, middle, out = refs[:10]
     else:
-        seg_smem, qkv, seg_row, seg_col, merge_hbm, out = refs[:6]
-    attended, merge_vmem, merge_sem = refs[-3:]
+        seg_smem, qkv_hbm, seg_row, seg_col, merge_hbm, out = refs[:6]
+    attended, merge_vmem, merge_sem, qkv, qkv_sem, turned_keys, turned_sides = refs[-7:]
     tiles = row_len // TILE
     edge_tiles = sent // TILE
     tokens = TILE // WIN
     fetch = pltpu.make_async_copy(merge_hbm, merge_vmem, merge_sem)
+    load = pltpu.make_async_copy(qkv_hbm, qkv, qkv_sem)
+    load.start()
     fetch.start()
+    if edge:
+        for side, source in enumerate((prev, following)):
+            for at in range(0, sent, TILE):
+                turned_sides[side, at : at + TILE, :] = source[0, :width, at : at + TILE].T
+    load.wait()
+
+    @pl.loop(0, tiles)
+    def _(tile):
+        at = pl.multiple_of(tile * TILE, TILE)
+        turned_keys[pl.ds(at, TILE), :] = qkv[1, :, pl.ds(at, TILE)].T
+
     ordered = lax.broadcasted_iota(jnp.int32, (TILE, TILE), 0)
     ordered = (ordered % tokens) * WIN + ordered // tokens
     order = (ordered == lax.broadcasted_iota(jnp.int32, (TILE, TILE), 1)).astype(jnp.float32)
@@ -93,14 +109,14 @@
             key_at = pl.multiple_of(jnp.minimum(begin, tiles - count) * TILE, TILE)
             key_ids = seg_col[pl.ds(key_at, count * TILE), :]
             bias_parts = [jnp.where(key_ids == query_ids, 0.0, NEG)]
-            key_parts = [lambda a, b: qkv[1, a:b, pl.ds(key_at, count * TILE)]]
+            key_parts = [lambda a, b: turned_keys[pl.ds(key_at, count * TILE), a:b]]
             value_parts = [lambda a, b: qkv[2, a:b, pl.ds(key_at, count * TILE)]]
             if neighbour is not None:
-                source, segment, open_link = neighbour
+                side, source, segment, open_link = neighbour
                 marks = jnp.transpose(source[0, width : width + PACK, :].astype(jnp.float32))[:, :1]
                 wanted = jnp.logical_and(query_ids == segment, open_link).astype(jnp.float32)
                 bias_parts.append(jnp.where(marks * wanted > 0.5, 0.0, NEG))
-                key_parts.append(lambda a, b: source[0, a:b, :])
+                key_parts.append(lambda a, b: turned_sides[side, :, a:b])
                 value_parts.append(lambda a, b: source[1, a:b, :])
             mixed = attend_heads(
                 width,
@@ -127,14 +143,14 @@
     if edge:
         @pl.loop(0, edge_tiles)
         def _(tile):
-            one(tile, pl.multiple_of(tile * tokens, tokens), (prev, seg_smem[0, 0], True))
+            one(tile, pl.multiple_of(tile * tokens, tokens), (0, prev, seg_smem[0, 0], True))
 
         @pl.loop(0, edge_tiles)
         def _(step):
             one(
                 tiles - edge_tiles + step,
                 pl.multiple_of((edge_tiles + step) * tokens, tokens),
-                (following, seg_smem[0, row_len - 1], links[0] > 0),
+                (1, following, seg_smem[0, row_len - 1], links[0] > 0),
             )
     else:
         @pl.loop(edge_tiles, tiles - edge_tiles)
@@ -167,7 +183,8 @@
         segments.reshape(row_len, 1),
         merge_weight,
     ]
-    specs = [smem, vmem, vmem, vmem, pl.BlockSpec(memory_space=pl.ANY)]
+    hbm = pl.BlockSpec(memory_space=pltpu.HBM)
+    specs = [smem, hbm, vmem, vmem, hbm]
     if edge:
         operands += list(extra)
         specs += [smem, vmem, vmem, vmem]
@@ -181,8 +198,12 @@
             pltpu.VMEM((WIN, rows // WIN, width), jnp.bfloat16),
             pltpu.VMEM(merge_weight.shape, jnp.bfloat16),
             pltpu.SemaphoreType.DMA,
+            pltpu.VMEM(qkv.shape, jnp.bfloat16),
+            pltpu.SemaphoreType.DMA,
+            pltpu.VMEM((row_len, width), jnp.bfloat16),
+            pltpu.VMEM((2, sent, width), jnp.bfloat16),
         ],
-        compiler_params=pltpu.CompilerParams(vmem_limit_bytes=28 << 20),
+        compiler_params=pltpu.CompilerParams(vmem_limit_bytes=40 << 20),
         cost_estimate=pl.CostEstimate(
             flops=rows * 512 * width * 6, bytes_accessed=qkv.size * 2, transcendentals=rows * 512 * 8
         ),
@@ -254,7 +275,7 @@
         ],
         out_specs=pl.BlockSpec((step, slots), lambda i: (i, 0)),
         scratch_shapes=[pltpu.VMEM((slots, model_width), jnp.bfloat16)],
-        compiler_params=pltpu.CompilerParams(vmem_limit_bytes=32 << 20),
+        compiler_params=pltpu.CompilerParams(vmem_limit_bytes=56 << 20),
         name="project",
     )(half, mine, other, weight)
 

time: 103 us -> 98.1 us (0.952); the launches traced: 101 us -> 98.3 us
  Pallas kernels: 33.8 us -> 28 us
  waiting for transfers between devices: 17.8 us -> 22.2 us
  local copies, waits for them, and re-layouts: 11.3 us -> 9.47 us
    pallas_call x2, Pallas kernels: 27.3 us -> 18.6 us  [run_attention(): pl.pallas_call(functools.partial(attention_kernel, edge, row_len, width,...]
    ppermute x2, waiting for transfers between devices: 12.7 us -> 17.1 us  [shifted(): return lax.ppermute(block, axis, route)]
    pallas_call x1, Pallas kernels: 5.52 us -> 8.43 us  [project(): pl.pallas_call(project_kernel, grid=(columns // step,), out_shape=jax.Sha...]
    unnamed x14 -> x16, local copies, waits for them, and re-layouts: 8.18 us -> 6.39 us
  transfers between devices with their start and end apart: 4 -> 4, of which waited for: 4 -> 4; matrix products, arithmetic and copies ran while one was open for 1% -> 2% of each run, Pallas kernels for 13% -> 9%
where the time goes in v3:
time: 98.1 us; the launch traced here: 98.3 us
  blocking collectives  29 us (30%)
  Pallas kernels  28 us (29%)
  waiting for transfers between devices  22.2 us (23%)
  local copies, waits for them, and re-layouts  9.47 us (10%)
  starting transfers between devices  6.24 us (6%)
  other arithmetic  2.58 us (3%)
    all_to_all x1, blocking collectives, body(): lax.all_to_all(packed, 'grp', split_axis=0, concat_axis=0, tiled=True)  29 us
    pallas_call x2, Pallas kernels, run_attention(): pl.pallas_call(functools.partial(attention_kernel, edge, row_len, width,...  18.6 us
    ppermute x2, waiting for transfers between devices, shifted(): return lax.ppermute(block, axis, route)  17.1 us
    pallas_call x1, Pallas kernels, project(): pl.pallas_call(project_kernel, grid=(columns // step,), out_shape=jax.Sha...  8.43 us
    unnamed x16, local copies, waits for them, and re-layouts  6.39 us
    ppermute x2, starting transfers between devices, shifted(): return lax.ppermute(block, axis, route)  6.17 us
    ppermute x2, waiting for transfers between devices, swapped(): return lax.ppermute(block, axis, [(0, 1), (1, 0)])  5.09 us
  transfers between devices with their start and end apart: 4, of which 4 were waited for; matrix products, arithmetic and copies ran while one was open for 2% of the time, Pallas kernels for 9%

profile of v3, /device:TPU:0, one launch (start us, length us, event | category | flops | bytes accessed | tf_op | source)
XLA Modules:
  0.0 98.3 jit_solution(15163912495104541564)
XLA Ops:
  0.0 0.0 copy-start.2
  0.0 1.3 %fusion.4 = (s32[1,1]{1,0:T(1,128)}, s32[1,1]{1,0:T(1,128)}) fusion(s32[1,1024]{1,0:T(1,128)} %refs_0_.3), kind=kLoop, calls=%fused_computation.12 | loop fusion | bytes 16 | tf_op jit(solution)/shard_map/slice | solution.py:291
  2.0 1.4 %fusion.3 = (bf16[2,704,256]{2,1,0:T(8,128)(2,1)S(1)}, bf16[2,704,256]{2,1,0:T(8,128)(2,1)S(1)}) fusion(bf16[3,704,1024]{2,1,0:T(8,128)(2,1)} %bitcast.15), kind=kLoop, calls=%fused_computation.11 | loop fusion | bytes 2883584 | tf_op jit(solution)/shard_map/slice | solution.py:299
  3.4 0.0 copy-done.2
  3.4 1.4 %fusion.1 = (bf16[256]{0:T(256)(128)(2,1)S(1)}, bf16[256]{0:T(256)(128)(2,1)S(1)}) fusion(s32[1,1024]{1,0:T(1,128)S(1)} %copy-done.2, s32[]{:T(128)} %bitcast.6, pred[]{:T(512)} %bitcast.5, s32[]{:T(128)} %bitcast.4), kind=kLoop, calls=%fused_computation.8 | loop fusion | flops 1280 | bytes 3081 | tf_op jit(solution)/shard_map/convert_element_type | solution.py:295
  4.8 0.1 pad_maximum_fusion
  4.9 4.9 %collective-permute-start = (bf16[2,720,256]{2,1,0:T(8,128)(2,1)S(1)}, bf16[2,720,256]{2,1,0:T(8,128)(2,1)S(1)}, u32[]{:S(2)}, u32[]{:S(2)}) collective-permute-start(bf16[2,720,256]{2,1,0:T(8,128)(2,1)S(1)} %pad_maximum_fusion), channel_id=1, source_target_pairs={{0,2},{2,4},{4,6},{6,8},{8,10},{10,12},{12,14},{14,16},{16,18},{18... | collective-permute-start | bytes 2211848 | tf_op jit(solution)/shard_map/ppermute | solution.py:24
  9.8 0.9 pad_maximum_fusion.1
  10.7 1.3 %collective-permute-start.1 = (bf16[2,720,256]{2,1,0:T(8,128)(2,1)}, bf16[2,720,256]{2,1,0:T(8,128)(2,1)S(1)}, u32[]{:S(2)}, u32[]{:S(2)}) collective-permute-start(bf16[2,720,256]{2,1,0:T(8,128)(2,1)} %pad_maximum_fusion.1), channel_id=1, source_target_pairs={{2,0},{4,2},{6,4},{8,6},{10,8},{12,10},{14,12},{16,14},{18,16},{20... | collective-permute-start | bytes 2211848 | tf_op jit(solution)/shard_map/ppermute | solution.py:24
  12.0 0.2 copy.12.refs_3_
  12.2 0.0 copy-start
  12.2 3.2 %copy-done = bf16[4,704,1408]{2,1,0:T(8,128)(2,1)S(1)} copy-done((bf16[4,704,1408]{2,1,0:T(8,128)(2,1)S(1)}, bf16[4,704,1408]{2,1,0:T(8,128)(2,1)}, u32[]{:S(2)}) %copy-start) | copy-done | bytes 7929880
  15.5 0.0 copy-start.1
  15.5 2.2 %copy-done.1 = bf16[3,1024,704]{1,2,0:T(8,128)(2,1)S(1)} copy-done((bf16[3,1024,704]{1,2,0:T(8,128)(2,1)S(1)}, bf16[3,1024,704]{1,2,0:T(8,128)(2,1)}, u32[]{:S(2)}) %copy-start.1) | copy-done | bytes 4325400
  17.7 8.4 %middle_attention.1.refs_8_ = f32[128,1408]{1,0:T(8,128)S(1)} custom-call(s32[1,1024]{1,0:T(1,128)S(1)} %copy-done.2, bf16[3,704,1024]{2,1,0:T(8,128)(2,1)S(1)} %bitcast.16, s32[8,128]{1,0:T(8,128)S(1)} %bitcast.20, s32[1024,1]{1,0:T(8,128)S(1)} %copy.12.refs_3_, bf16[4,704,1408]{2,1,0:T(8,128)(2,1)S(1)} %copy-done), custom_call_target="tpu_custom_call" | custom-call | flops 1107296256 | bytes 4325376 | tf_op jit(solution)/shard_map/middle_attention/pallas_call | solution.py:192
  26.1 0.0 copy-start.7
  26.1 0.0 copy-start.5
  26.1 0.0 copy-start.6
  26.1 15.1 %collective-permute-done.refs_6_ = bf16[2,720,256]{2,1,0:T(8,128)(2,1)S(1)} collective-permute-done((bf16[2,720,256]{2,1,0:T(8,128)(2,1)S(1)}, bf16[2,720,256]{2,1,0:T(8,128)(2,1)S(1)}, u32[]{:S(2)}, u32[]{:S(2)}) %collective-permute-start) | collective-permute-done | bytes 737312 | tf_op jit(solution)/shard_map/ppermute | solution.py:24
  41.2 1.9 %collective-permute-done.1.refs_7_ = bf16[2,720,256]{2,1,0:T(8,128)(2,1)S(1)} collective-permute-done((bf16[2,720,256]{2,1,0:T(8,128)(2,1)}, bf16[2,720,256]{2,1,0:T(8,128)(2,1)S(1)}, u32[]{:S(2)}, u32[]{:S(2)}) %collective-permute-start.1) | collective-permute-done | bytes 737312 | tf_op jit(solution)/shard_map/ppermute | solution.py:24
  43.2 10.2 %edge_attention.1.mine_ref = f32[256,1408]{1,0:T(8,128)S(1)} custom-call(s32[1,1024]{1,0:T(1,128)S(1)} %copy-done.2, bf16[3,704,1024]{2,1,0:T(8,128)(2,1)S(1)} %bitcast.17, s32[8,128]{1,0:T(8,128)S(1)} %bitcast.21, s32[1024,1]{1,0:T(8,128)S(1)} %copy.12.refs_3_, bf16[4,704,1408]{2,1,0:T(8,128)(2,1)} %refs_4_.3, s32[1]{0:T(128)S(6)} %copy.13.refs_5_, ...), custom_call_target="tpu_custom_call" | custom-call | flops 1107296256 | bytes 4325376 | tf_op jit(solution)/shard_map/edge_attention/pallas_call | solution.py:192
  53.4 0.1 collective-permute-start.2
  53.5 0.0 copy-done.7
  53.5 0.2 convert_reduce_fusion
  53.7 0.1 iota_add_fusion
  53.7 0.1 add.31.target_ref
  53.8 0.0 copy-done.5
  53.8 0.0 copy-done.6
  53.9 2.8 %collective-permute-done.2.other_ref = f32[256,1408]{1,0:T(8,128)S(1)} collective-permute-done((f32[256,1408]{1,0:T(8,128)S(1)}, f32[256,1408]{1,0:T(8,128)S(1)}, u32[]{:S(2)}, u32[]{:S(2)}) %collective-permute-start.2) | collective-permute-done | bytes 1441824 | tf_op jit(solution)/shard_map/ppermute | solution.py:28
  56.7 1.0 norm_pack.1
  57.6 29.0 %all_to_all.5 = bf16[16,32,768]{2,1,0:T(8,128)(2,1)S(1)} all-to-all(bf16[16,32,768]{2,1,0:T(8,128)(2,1)S(1)} %bitcast.18), channel_id=1, replica_groups=mesh['grp'=16,'tp'=2] {'grp'}, dimensions={0} | all-to-all | bytes 1572864 | tf_op jit(solution)/shard_map/all_to_all | solution.py:327
  86.7 0.0 copy-start.3
  86.7 0.0 collective-permute-start.3
  86.7 2.3 %collective-permute-done.3.other_ref = bf16[512,768]{1,0:T(8,128)(2,1)S(1)} collective-permute-done((bf16[512,768]{1,0:T(8,128)(2,1)S(1)}, bf16[512,768]{1,0:T(8,128)(2,1)S(1)}, u32[]{:S(2)}, u32[]{:S(2)}) %collective-permute-start.3) | collective-permute-done | bytes 786464 | tf_op jit(solution)/shard_map/ppermute | solution.py:28
  89.0 0.0 copy-start.4
  89.0 0.0 copy-done.3
  89.0 0.9 copy-done.4
  89.9 8.4 %project.1 = bf16[2112,512]{1,0:T(8,128)(2,1)} custom-call(s32[1]{0:T(128)} %bitcast.half_ref, bf16[512,768]{1,0:T(8,128)(2,1)} %bitcast.24, bf16[512,768]{1,0:T(8,128)(2,1)} %copy-done.4, bf16[2112,1408]{1,0:T(8,128)(2,1)} %bitcast.22), custom_call_target="tpu_custom_call" | custom-call | tf_op jit(solution)/shard_map/project/pallas_call | solution.py:266
  (5 shorter events, 0.0 us)
Async XLA Ops:
  0.0 3.4 %copy-start.2 = (s32[1,1024]{1,0:T(1,128)S(1)}, s32[1,1024]{1,0:T(1,128)}, u32[]{:S(2)}) copy-start(s32[1,1024]{1,0:T(1,128)} %refs_0_.3) | copy-start | bytes 12292
  4.9 36.4 %collective-permute-start = (bf16[2,720,256]{2,1,0:T(8,128)(2,1)S(1)}, bf16[2,720,256]{2,1,0:T(8,128)(2,1)S(1)}, u32[]{:S(2)}, u32[]{:S(2)}) collective-permute-start(bf16[2,720,256]{2,1,0:T(8,128)(2,1)S(1)} %pad_maximum_fusion), channel_id=1, source_target_pairs={{0,2},{2,4},{4,6},{6,8},{8,10},{10,12},{12,14},{14,16},{16,18},{18... | collective-permute-start | bytes 2211848 | tf_op jit(solution)/shard_map/ppermute | solution.py:24
  10.7 32.5 %collective-permute-start.1 = (bf16[2,720,256]{2,1,0:T(8,128)(2,1)}, bf16[2,720,256]{2,1,0:T(8,128)(2,1)S(1)}, u32[]{:S(2)}, u32[]{:S(2)}) collective-permute-start(bf16[2,720,256]{2,1,0:T(8,128)(2,1)} %pad_maximum_fusion.1), channel_id=1, source_target_pairs={{2,0},{4,2},{6,4},{8,6},{10,8},{12,10},{14,12},{16,14},{18,16},{20... | collective-permute-start | bytes 2211848 | tf_op jit(solution)/shard_map/ppermute | solution.py:24
  12.2 3.3 %copy-start = (bf16[4,704,1408]{2,1,0:T(8,128)(2,1)S(1)}, bf16[4,704,1408]{2,1,0:T(8,128)(2,1)}, u32[]{:S(2)}) copy-start(bf16[4,704,1408]{2,1,0:T(8,128)(2,1)} %refs_4_.3) | copy-start | bytes 23789572
  15.5 2.2 %copy-start.1 = (bf16[3,1024,704]{1,2,0:T(8,128)(2,1)S(1)}, bf16[3,1024,704]{1,2,0:T(8,128)(2,1)}, u32[]{:S(2)}) copy-start(bf16[3,1024,704]{1,2,0:T(8,128)(2,1)} %param.8) | copy-start | bytes 12976132
  26.1 27.4 %copy-start.7 = (s32[1,16,1]{1,2,0:T(1,128)S(1)}, s32[1,16,1]{1,2,0:T(1,128)}, u32[]{:S(2)}) copy-start(s32[1,16,1]{1,2,0:T(1,128)} %param.11) | copy-start | bytes 196
  26.1 27.7 %copy-start.5 = (f32[1408]{0:T(1024)S(1)}, f32[1408]{0:T(1024)}, u32[]{:S(2)}) copy-start(f32[1408]{0:T(1024)} %param.13) | copy-start | bytes 16900
  26.1 27.7 %copy-start.6 = (f32[1408]{0:T(1024)S(1)}, f32[1408]{0:T(1024)}, u32[]{:S(2)}) copy-start(f32[1408]{0:T(1024)} %param.14) | copy-start | bytes 16900
  53.4 3.3 %collective-permute-start.2 = (f32[256,1408]{1,0:T(8,128)S(1)}, f32[256,1408]{1,0:T(8,128)S(1)}, u32[]{:S(2)}, u32[]{:S(2)}) collective-permute-start(f32[256,1408]{1,0:T(8,128)S(1)} %edge_attention.1.mine_ref), channel_id=1, source_target_pairs={{0,1},{1,0},{2,3},{3,2},{4,5},{5,4},{6,7},{7,6},{8,9},{9,8},{10,11... | collective-permute-start | bytes 4325384 | tf_op jit(solution)/shard_map/ppermute | solution.py:28
  86.7 2.3 %copy-start.3 = (bf16[16,32,768]{2,1,0:T(8,128)(2,1)}, bf16[16,32,768]{2,1,0:T(8,128)(2,1)S(1)}, u32[]{:S(2)}) copy-start(bf16[16,32,768]{2,1,0:T(8,128)(2,1)S(1)} %all_to_all.5) | copy-start | bytes 2359300
  86.7 2.3 %collective-permute-start.3 = (bf16[512,768]{1,0:T(8,128)(2,1)S(1)}, bf16[512,768]{1,0:T(8,128)(2,1)S(1)}, u32[]{:S(2)}, u32[]{:S(2)}) collective-permute-start(bf16[512,768]{1,0:T(8,128)(2,1)S(1)} %bitcast.23), channel_id=1, source_target_pairs={{0,1},{1,0},{2,3},{3,2},{4,5},{5,4},{6,7},{7,6},{8,9},{9,8},{10,11... | collective-permute-start | bytes 2359304 | tf_op jit(solution)/shard_map/ppermute | solution.py:28
  89.0 0.9 copy-start.4
